TPU v7x, 256 devices: a whole 4x4x8 slice. The times are simulated.
256 devices in a mesh: freq: 16 (over x, z_hi), tile: 16 (over z_lo, y, core).
Axes of the slice: x: 4, y: 4, z: 8 (z_hi: 4, z_lo: 2; z = z_hi * 2 + z_lo), core: 2. Of those that a mesh axis runs over, the one named last changes fastest.
Arguments:
- sky_cube: float32 [256, 256, 128], P(('freq', 'tile')), may hold values from -6 to 6
- kernel_one: bfloat16 [8, 1, 3, 3, 3], replicated, may hold values from -1.25 to 1.25
- bias_one: float32 [8], replicated, may hold values from -2 to 2
- kernel_two: bfloat16 [8, 8, 3, 3, 3], replicated, may hold values from -0.4375 to 0.4375
- bias_two: float32 [8], replicated, may hold values from -2 to 2
- kernel_three: bfloat16 [16, 8, 3, 3, 3], replicated, may hold values from -0.4375 to 0.4375
- bias_three: float32 [16], replicated, may hold values from -2 to 2
Outputs:
- features: bfloat16 [16, 128, 128, 64], P(None, 'freq', 'tile')
All inputs are finite; a program needn't handle non-finite values.
Results may differ from a plain program's by a relative error of at most 0.0066.
Values may be sent and summed in bfloat16 or wider, within the bound.
A program may use at most 64 MiB of HBM per device.

v0:
```python
import jax
import jax.numpy as jnp
from jax import lax
from jax.sharding import PartitionSpec as P


def extended_2(cells, sides, width):
    for axis, dim in sides:
        count = lax.axis_size(axis)
        ends = count - 1
        head = lax.slice_in_dim(cells, 0, width, axis=dim)
        tail = lax.slice_in_dim(cells, cells.shape[dim] - width, cells.shape[dim], axis=dim)
        cells = jnp.concatenate(
            [
                lax.ppermute(tail, axis, [(i, (i + 1) % count) for i in range(ends)]),
                cells,
                lax.ppermute(head, axis, [((i + 1) % count, i) for i in range(ends)]),
            ],
            axis=dim,
        )
    return cells


def shortened(shard):

    def short(part):
        return part.astype(jnp.bfloat16) if part.dtype == jnp.float32 else part

    return jax.tree.map(short, shard)


def from_behind(shard, axis, by):
    devices = lax.axis_size(axis)
    pairs = [(i, i + by) for i in range(devices) if 0 <= i + by < devices]
    return lax.ppermute(shard, axis, pairs)


def leaky_relu(values):
    return jnp.maximum(values, 0.1 * values)


def conv_layer(volume, kernel, bias_term):
    depth = volume.shape[1] - 2
    blocks = []
    for begin_at in range(0, depth, 4):
        count = min(4, depth - begin_at)
        section = volume[:, begin_at : begin_at + count + 2]
        values = lax.conv_general_dilated(
            section[None],
            kernel,
            (1, 1, 1),
            ((0, 0), (0, 0), (1, 1)),
            dimension_numbers=("NCDHW", "OIDHW", "NCDHW"),
            preferred_element_type=jnp.float32,
        )[0]
        values = leaky_relu(values + bias_term[:, None, None, None])
        blocks.append(values.astype(jnp.bfloat16))
    return jnp.concatenate(blocks, axis=1)


def body(sky_cube, kernel_one, bias_one, kernel_two, bias_two, kernel_three, bias_three):
    slab = lax.all_to_all(
        sky_cube.astype(jnp.bfloat16), "tile", split_axis=1, concat_axis=0, tiled=True
    )
    widened = extended_2(slab, (("freq", 0), ("tile", 1)), 1)
    layer_one = conv_layer(widened[None], kernel_one, bias_one)
    widened = extended_2(layer_one, (("freq", 1), ("tile", 2)), 1)
    layer_two = conv_layer(widened, kernel_two, bias_two)
    lower_rows = from_behind(shortened(layer_two[:, :, -1:, :]), "tile", 1)
    extended = jnp.concatenate([lower_rows, layer_two], axis=2)
    lower_planes = from_behind(shortened(extended[:, -1:]), "freq", 1)
    extended = jnp.concatenate([lower_planes, extended], axis=1)
    values = lax.conv_general_dilated(
        extended[None],
        kernel_three,
        (2, 2, 2),
        ((0, 0), (0, 0), (1, 1)),
        dimension_numbers=("NCDHW", "OIDHW", "NCDHW"),
        preferred_element_type=jnp.float32,
    )[0]
    return leaky_relu(values + bias_three[:, None, None, None]).astype(jnp.bfloat16)


def solution(mesh):
    return jax.shard_map(
        body,
        mesh=mesh,
        in_specs=(P(("freq", "tile"), None, None), P(), P(), P(), P(), P(), P()),
        out_specs=P(None, "freq", "tile", None),
        check_vma=False,
    )
```

profile of v0, /device:TPU:34, one launch (start us, length us, event | category | flops | bytes accessed | tf_op | source)
XLA Modules:
  0.0 293.1 jit_solution(5028507617221354503)
XLA Ops:
  2.6 10.6 %all_to_all.15 = bf16[16,2,1024]{2,1,0:T(2,128)(2,1)S(1)} all-to-all(bf16[16,2,1024]{2,1,0:T(2,128)(2,1)S(1)} %reshape.116), channel_id=1, replica_groups=mesh['freq'=16,'tile'=16] {'tile'}, dimensions={0} | all-to-all | bytes 131072 | tf_op jit(solution)/shard_map/all_to_all | solution.py:62
  27.5 5.8 %collective-permute-start.3 = (bf16[18,1,128]{2,1,0:T(2,128)(2,1)S(1)}, bf16[18,1,128]{2,1,0:T(2,128)(2,1)S(1)}, u32[]{:S(2)}, u32[]{:S(2)}) collective-permute-start(bf16[18,1,128]{2,1,0:T(2,128)(2,1)S(1)} %get-tuple-element.18), channel_id=1, source_target_pairs={{1,0},{2,1},{3,2},{4,3},{5,4},{6,5},{7,6},{8,7},{9,8},{10,9},{11,1... | collective-permute-start | bytes 13832 | tf_op jit(solution)/shard_map/ppermute | solution.py:17
  44.7 8.6 %broadcast_select_fusion.4 = f32[4,16,8,17,8]{4,2,3,1,0:T(8,128)} fusion(pred[8,17]{0,1:T(8,128)(4,1)S(1)} %copy-done.6, bf16[1,6,18,8,19]{3,0,4,2,1:T(2,128)(2,1)S(1)} %copy.151, bf16[8,1,3,3,3]{0,4,3,2,1:T(4,128)(2,1)S(1)} %copy-done.5), kind=kOutput, calls=%fused_computation.39 | convolution fusion | flops 3829760 | bytes 311928 | tf_op jit(solution)/shard_map/conv_general_dilated | solution.py:48
  53.3 8.7 %broadcast_select_fusion.5 = f32[4,16,8,17,8]{4,2,3,1,0:T(8,128)} fusion(pred[8,17]{0,1:T(8,128)(4,1)S(1)} %copy-done.6, bf16[1,6,18,8,19]{3,0,4,2,1:T(2,128)(2,1)S(1)} %copy.148, bf16[8,1,3,3,3]{0,4,3,2,1:T(4,128)(2,1)S(1)} %copy-done.5), kind=kOutput, calls=%fused_computation.40 | convolution fusion | flops 3829760 | bytes 311928 | tf_op jit(solution)/shard_map/conv_general_dilated | solution.py:48
  62.1 8.8 %broadcast_select_fusion.7 = f32[4,16,8,17,8]{4,2,3,1,0:T(8,128)} fusion(pred[8,17]{0,1:T(8,128)(4,1)S(1)} %copy-done.6, bf16[1,6,18,8,19]{3,0,4,2,1:T(2,128)(2,1)S(1)} %copy.142, bf16[8,1,3,3,3]{0,4,3,2,1:T(4,128)(2,1)S(1)} %copy-done.5), kind=kOutput, calls=%fused_computation.42 | convolution fusion | flops 3829760 | bytes 311928 | tf_op jit(solution)/shard_map/conv_general_dilated | solution.py:48
  70.8 5.7 %copy.144 = f32[4,16,8,17,8]{3,2,4,1,0:T(8,128)S(1)} copy(f32[4,16,8,17,8]{4,2,3,1,0:T(8,128)} %broadcast_select_fusion.7) | data formatting | bytes 557056 | tf_op jit(solution)/shard_map/conv_general_dilated | solution.py:48
  77.3 6.0 %collective-permute-start.4 = (bf16[8,1,16,128]{3,0,2,1:T(8,128)(2,1)S(1)}, bf16[8,1,16,128]{3,0,2,1:T(8,128)(2,1)S(1)}, u32[]{:S(2)}, u32[]{:S(2)}) collective-permute-start(bf16[8,1,16,128]{3,0,2,1:T(8,128)(2,1)S(1)} %slice.100), channel_id=1, source_target_pairs={{0,16},{16,32},{32,48},{48,64},{64,80},{80,96},{96,112},{112,128},... | collective-permute-start | bytes 98312 | tf_op jit(solution)/shard_map/ppermute | solution.py:15
  83.3 9.6 %broadcast_select_fusion.6 = f32[4,16,8,17,8]{4,2,3,1,0:T(8,128)} fusion(pred[8,17]{0,1:T(8,128)(4,1)S(1)} %copy-done.6, bf16[1,6,18,8,19]{3,0,4,2,1:T(2,128)(2,1)} %copy.145, bf16[8,1,3,3,3]{0,4,3,2,1:T(4,128)(2,1)S(1)} %copy-done.5), kind=kOutput, calls=%fused_computation.41 | convolution fusion | flops 3829760 | bytes 311928 | tf_op jit(solution)/shard_map/conv_general_dilated | solution.py:48
  120.6 5.8 %collective-permute-start.7 = (bf16[8,18,1,128]{3,0,2,1:T(8,128)(2,1)S(1)}, bf16[8,18,1,128]{3,0,2,1:T(8,128)(2,1)S(1)}, u32[]{:S(2)}, u32[]{:S(2)}) collective-permute-start(bf16[8,18,1,128]{3,0,2,1:T(8,128)(2,1)S(1)} %get-tuple-element.12), channel_id=1, source_target_pairs={{1,0},{2,1},{3,2},{4,3},{5,4},{6,5},{7,6},{8,7},{9,8},{10,9},{11,1... | collective-permute-start | bytes 110600 | tf_op jit(solution)/shard_map/ppermute | solution.py:17
  137.2 6.7 %copy.155 = bf16[8,6,18,1,8,17]{0,4,5,2,1,3:T(8,128)(2,1)} copy(bf16[8,6,18,1,8,17]{5,4,0,2,1,3:T(8,128)(2,1)S(1)} %reshape.38) | data formatting | bytes 470016 | tf_op jit(solution)/shard_map/conv_general_dilated | solution.py:48
  145.0 9.7 %broadcast_select_fusion.3 = f32[4,16,8,17,8]{4,2,3,1,0:T(8,128)} fusion(pred[8,17]{0,1:T(8,128)(4,1)S(1)} %copy-done.6, bf16[8,8,3,3,3]{1,0,4,3,2:T(8,128)(2,1)S(1)} %copy-done, bf16[8,6,18,1,7,2]{0,4,5,2,1,3:T(8,128)(2,1)S(1)} %slice.114, bf16[8,6,18,1,8,17]{0,4,5,2,1,3:T(8,128)(2,1)} %copy.155), kind=kOutput, calls=%fused_computation.38 | convolution fusion | flops 30938624 | bytes 541320 | tf_op jit(solution)/shard_map/conv_general_dilated | solution.py:48
  160.5 7.5 %copy.164 = bf16[8,6,18,1,8,17]{0,4,5,2,1,3:T(8,128)(2,1)} copy(bf16[8,6,18,1,8,17]{5,4,0,2,1,3:T(8,128)(2,1)} %reshape.59) | data formatting | bytes 470016 | tf_op jit(solution)/shard_map/conv_general_dilated | solution.py:48
  169.2 9.7 %broadcast_select_fusion = f32[4,16,8,17,8]{4,2,3,1,0:T(8,128)} fusion(pred[8,17]{0,1:T(8,128)(4,1)S(1)} %copy-done.6, bf16[8,8,3,3,3]{1,0,4,3,2:T(8,128)(2,1)S(1)} %copy-done, bf16[8,6,18,1,7,2]{0,4,5,2,1,3:T(8,128)(2,1)S(1)} %slice.123, bf16[8,6,18,1,8,17]{0,4,5,2,1,3:T(8,128)(2,1)} %copy.164), kind=kOutput, calls=%fused_computation.35 | convolution fusion | flops 30938624 | bytes 541320 | tf_op jit(solution)/shard_map/conv_general_dilated | solution.py:48
  179.0 5.4 %copy.165 = f32[4,16,8,17,8]{3,2,4,1,0:T(8,128)S(1)} copy(f32[4,16,8,17,8]{4,2,3,1,0:T(8,128)} %broadcast_select_fusion) | data formatting | bytes 557056 | tf_op jit(solution)/shard_map/conv_general_dilated | solution.py:48
  184.9 7.5 %copy.161 = bf16[8,6,18,1,8,17]{0,4,5,2,1,3:T(8,128)(2,1)} copy(bf16[8,6,18,1,8,17]{5,4,0,2,1,3:T(8,128)(2,1)} %reshape.52) | data formatting | bytes 470016 | tf_op jit(solution)/shard_map/conv_general_dilated | solution.py:48
  193.6 9.7 %broadcast_select_fusion.1 = f32[4,16,8,17,8]{4,2,3,1,0:T(8,128)} fusion(pred[8,17]{0,1:T(8,128)(4,1)S(1)} %copy-done.6, bf16[8,8,3,3,3]{1,0,4,3,2:T(8,128)(2,1)S(1)} %copy-done, bf16[8,6,18,1,7,2]{0,4,5,2,1,3:T(8,128)(2,1)S(1)} %slice.120, bf16[8,6,18,1,8,17]{0,4,5,2,1,3:T(8,128)(2,1)} %copy.161), kind=kOutput, calls=%fused_computation.36 | convolution fusion | flops 30938624 | bytes 541320 | tf_op jit(solution)/shard_map/conv_general_dilated | solution.py:48
  209.9 7.5 %copy.158 = bf16[8,6,18,1,8,17]{0,4,5,2,1,3:T(8,128)(2,1)} copy(bf16[8,6,18,1,8,17]{5,4,0,2,1,3:T(8,128)(2,1)} %reshape.45) | data formatting | bytes 470016 | tf_op jit(solution)/shard_map/conv_general_dilated | solution.py:48
  218.6 9.7 %broadcast_select_fusion.2 = f32[4,16,8,17,8]{4,2,3,1,0:T(8,128)} fusion(pred[8,17]{0,1:T(8,128)(4,1)S(1)} %copy-done.6, bf16[8,8,3,3,3]{1,0,4,3,2:T(8,128)(2,1)S(1)} %copy-done, bf16[8,6,18,1,7,2]{0,4,5,2,1,3:T(8,128)(2,1)S(1)} %slice.117, bf16[8,6,18,1,8,17]{0,4,5,2,1,3:T(8,128)(2,1)} %copy.158), kind=kOutput, calls=%fused_computation.37 | convolution fusion | flops 30938624 | bytes 541320 | tf_op jit(solution)/shard_map/conv_general_dilated | solution.py:48
  228.4 5.2 %copy.159 = f32[4,16,8,17,8]{3,2,4,1,0:T(8,128)S(1)} copy(f32[4,16,8,17,8]{4,2,3,1,0:T(8,128)} %broadcast_select_fusion.2) | data formatting | bytes 557056 | tf_op jit(solution)/shard_map/conv_general_dilated | solution.py:48
  238.2 5.8 %collective-permute-done.8 = bf16[8,16,1,128]{3,0,2,1:T(8,128)(2,1)S(1)} collective-permute-done((bf16[8,16,1,128]{3,0,2,1:T(8,128)(2,1)S(1)}, bf16[8,16,1,128]{3,0,2,1:T(8,128)(2,1)S(1)}, u32[]{:S(2)}, u32[]{:S(2)}) %collective-permute-start.8) | collective-permute-done | bytes 32800 | tf_op jit(solution)/shard_map/ppermute | solution.py:35
  247.2 5.6 %collective-permute-done.9 = bf16[8,1,17,128]{3,0,2,1:T(8,128)(2,1)S(1)} collective-permute-done((bf16[8,1,17,128]{3,0,2,1:T(8,128)(2,1)S(1)}, bf16[8,1,17,128]{3,0,2,1:T(8,128)(2,1)S(1)}, u32[]{:S(2)}, u32[]{:S(2)}) %collective-permute-start.9) | collective-permute-done | bytes 34848 | tf_op jit(solution)/shard_map/ppermute | solution.py:35
  253.2 5.7 %reshape.66 = bf16[8,17,17,1,8,18]{5,4,0,2,1,3:T(8,128)(2,1)} reshape(bf16[8,17,17,1,144]{4,0,2,1,3:T(8,128)(2,1)S(1)} %pad.16) | data formatting | bytes 1331712 | tf_op jit(solution)/shard_map/conv_general_dilated | solution.py:73
  259.0 18.6 %copy.167 = bf16[8,17,17,1,8,18]{0,4,5,2,1,3:T(8,128)(2,1)} copy(bf16[8,17,17,1,8,18]{5,4,0,2,1,3:T(8,128)(2,1)} %reshape.66) | data formatting | bytes 1331712 | tf_op jit(solution)/shard_map/conv_general_dilated | solution.py:73
  279.2 11.3 %fusion.50 = f32[8,8,8,9,16]{4,2,3,1,0:T(8,128)S(1)} fusion(bf16[16,8,3,3,3]{0,1,4,3,2:T(8,128)(2,1)S(1)} %copy-done.4, bf16[8,17,17,1,7,2]{0,4,5,2,1,3:T(8,128)(2,1)S(1)} %slice.125, bf16[8,17,17,1,8,18]{0,4,5,2,1,3:T(8,128)(2,1)} %copy.167, pred[8,9]{0,1:T(8,128)(4,1)S(1)} %copy-done.7), kind=kOutput, calls=%fused_computation.47 | convolution fusion | flops 34143744 | bytes 1032488 | tf_op jit(solution)/shard_map/conv_general_dilated | solution.py:73
  (111 shorter events, 96.8 us)
Async XLA Ops:
  0.0 145.0 %copy-start = (bf16[8,8,3,3,3]{1,0,4,3,2:T(8,128)(2,1)S(1)}, bf16[8,8,3,3,3]{1,0,4,3,2:T(8,128)(2,1)}, u32[]{:S(2)}) copy-start(bf16[8,8,3,3,3]{1,0,4,3,2:T(8,128)(2,1)} %param.10) | copy-start | bytes 10372
  13.3 9.2 %collective-permute-start = (bf16[1,16,128]{2,1,0:T(8,128)(2,1)S(1)}, bf16[1,16,128]{2,1,0:T(8,128)(2,1)S(1)}, u32[]{:S(2)}, u32[]{:S(2)}) collective-permute-start(bf16[1,16,128]{2,1,0:T(8,128)(2,1)S(1)} %slice_bitcast_fusion.16), channel_id=1, source_target_pairs={{0,16},{16,32},{32,48},{48,64},{64,80},{80,96},{96,112},{112,128},... | collective-permute-start | bytes 12296 | tf_op jit(solution)/shard_map/ppermute | solution.py:15
  18.5 7.1 %collective-permute-start.1 = (bf16[1,16,128]{2,1,0:T(8,128)(2,1)S(1)}, bf16[1,16,128]{2,1,0:T(8,128)(2,1)S(1)}, u32[]{:S(2)}, u32[]{:S(2)}) collective-permute-start(bf16[1,16,128]{2,1,0:T(8,128)(2,1)S(1)} %copy.172), channel_id=1, source_target_pairs={{16,0},{32,16},{48,32},{64,48},{80,64},{96,80},{112,96},{128,112},... | collective-permute-start | bytes 12296 | tf_op jit(solution)/shard_map/ppermute | solution.py:17
  25.6 7.7 %collective-permute-start.2 = (bf16[18,1,128]{2,1,0:T(2,128)(2,1)S(1)}, bf16[18,1,128]{2,1,0:T(2,128)(2,1)S(1)}, u32[]{:S(2)}, u32[]{:S(2)}) collective-permute-start(bf16[18,1,128]{2,1,0:T(2,128)(2,1)S(1)} %get-tuple-element.17), channel_id=1, source_target_pairs={{0,1},{1,2},{2,3},{3,4},{4,5},{5,6},{6,7},{7,8},{8,9},{9,10},{10,1... | collective-permute-start | bytes 13832 | tf_op jit(solution)/shard_map/ppermute | solution.py:15
  27.5 7.1 %collective-permute-start.3 = (bf16[18,1,128]{2,1,0:T(2,128)(2,1)S(1)}, bf16[18,1,128]{2,1,0:T(2,128)(2,1)S(1)}, u32[]{:S(2)}, u32[]{:S(2)}) collective-permute-start(bf16[18,1,128]{2,1,0:T(2,128)(2,1)S(1)} %get-tuple-element.18), channel_id=1, source_target_pairs={{1,0},{2,1},{3,2},{4,3},{5,4},{6,5},{7,6},{8,7},{9,8},{10,9},{11,1... | collective-permute-start | bytes 13832 | tf_op jit(solution)/shard_map/ppermute | solution.py:17
  36.1 8.5 %copy-start.5 = (bf16[8,1,3,3,3]{0,4,3,2,1:T(4,128)(2,1)S(1)}, bf16[8,1,3,3,3]{0,4,3,2,1:T(4,128)(2,1)}, u32[]{:S(2)}) copy-start(bf16[8,1,3,3,3]{0,4,3,2,1:T(4,128)(2,1)} %param.8) | copy-start | bytes 1300
  36.1 8.5 %copy-start.6 = (pred[8,17]{0,1:T(8,128)(4,1)S(1)}, pred[8,17]{0,1:T(8,128)(4,1)}, u32[]{:S(2)}) copy-start(pred[8,17]{0,1:T(8,128)(4,1)} %constant.41) | copy-start | bytes 412
  70.8 6.3 %copy-start.1 = (f32[8]{0:T(128)S(1)}, f32[8]{0:T(128)}, u32[]{:S(2)}) copy-start(f32[8]{0:T(128)} %param.9) | copy-start | bytes 100
  77.3 34.5 %collective-permute-start.4 = (bf16[8,1,16,128]{3,0,2,1:T(8,128)(2,1)S(1)}, bf16[8,1,16,128]{3,0,2,1:T(8,128)(2,1)S(1)}, u32[]{:S(2)}, u32[]{:S(2)}) collective-permute-start(bf16[8,1,16,128]{3,0,2,1:T(8,128)(2,1)S(1)} %slice.100), channel_id=1, source_target_pairs={{0,16},{16,32},{32,48},{48,64},{64,80},{80,96},{96,112},{112,128},... | collective-permute-start | bytes 98312 | tf_op jit(solution)/shard_map/ppermute | solution.py:15
  112.0 6.7 %collective-permute-start.5 = (bf16[8,1,16,128]{3,0,2,1:T(8,128)(2,1)S(1)}, bf16[8,1,16,128]{3,0,2,1:T(8,128)(2,1)S(1)}, u32[]{:S(2)}, u32[]{:S(2)}) collective-permute-start(bf16[8,1,16,128]{3,0,2,1:T(8,128)(2,1)S(1)} %slice.110), channel_id=1, source_target_pairs={{16,0},{32,16},{48,32},{64,48},{80,64},{96,80},{112,96},{128,112},... | collective-permute-start | bytes 98312 | tf_op jit(solution)/shard_map/ppermute | solution.py:17
  118.7 7.7 %collective-permute-start.6 = (bf16[8,18,1,128]{3,0,2,1:T(8,128)(2,1)S(1)}, bf16[8,18,1,128]{3,0,2,1:T(8,128)(2,1)S(1)}, u32[]{:S(2)}, u32[]{:S(2)}) collective-permute-start(bf16[8,18,1,128]{3,0,2,1:T(8,128)(2,1)S(1)} %get-tuple-element.11), channel_id=1, source_target_pairs={{0,1},{1,2},{2,3},{3,4},{4,5},{5,6},{6,7},{7,8},{8,9},{9,10},{10,1... | collective-permute-start | bytes 110600 | tf_op jit(solution)/shard_map/ppermute | solution.py:15
  120.6 7.4 %collective-permute-start.7 = (bf16[8,18,1,128]{3,0,2,1:T(8,128)(2,1)S(1)}, bf16[8,18,1,128]{3,0,2,1:T(8,128)(2,1)S(1)}, u32[]{:S(2)}, u32[]{:S(2)}) collective-permute-start(bf16[8,18,1,128]{3,0,2,1:T(8,128)(2,1)S(1)} %get-tuple-element.12), channel_id=1, source_target_pairs={{1,0},{2,1},{3,2},{4,3},{5,4},{6,5},{7,6},{8,7},{9,8},{10,9},{11,1... | collective-permute-start | bytes 110600 | tf_op jit(solution)/shard_map/ppermute | solution.py:17
  228.4 6.6 %copy-start.2 = (f32[8]{0:T(128)S(1)}, f32[8]{0:T(128)}, u32[]{:S(2)}) copy-start(f32[8]{0:T(128)} %param.11) | copy-start | bytes 100
  236.2 7.7 %collective-permute-start.8 = (bf16[8,16,1,128]{3,0,2,1:T(8,128)(2,1)S(1)}, bf16[8,16,1,128]{3,0,2,1:T(8,128)(2,1)S(1)}, u32[]{:S(2)}, u32[]{:S(2)}) collective-permute-start(bf16[8,16,1,128]{3,0,2,1:T(8,128)(2,1)S(1)} %pad_maximum_fusion.5), channel_id=1, source_target_pairs={{0,1},{1,2},{2,3},{3,4},{4,5},{5,6},{6,7},{7,8},{8,9},{9,10},{10,1... | collective-permute-start | bytes 98312 | tf_op jit(solution)/shard_map/ppermute | solution.py:35
  244.0 8.8 %collective-permute-start.9 = (bf16[8,1,17,128]{3,0,2,1:T(8,128)(2,1)S(1)}, bf16[8,1,17,128]{3,0,2,1:T(8,128)(2,1)S(1)}, u32[]{:S(2)}, u32[]{:S(2)}) collective-permute-start(bf16[8,1,17,128]{3,0,2,1:T(8,128)(2,1)S(1)} %pad_maximum_fusion.1), channel_id=1, source_target_pairs={{0,16},{16,32},{32,48},{48,64},{64,80},{80,96},{96,112},{112,128},... | collective-permute-start | bytes 104456 | tf_op jit(solution)/shard_map/ppermute | solution.py:35
  259.0 20.3 %copy-start.4 = (bf16[16,8,3,3,3]{0,1,4,3,2:T(8,128)(2,1)S(1)}, bf16[16,8,3,3,3]{0,1,4,3,2:T(8,128)(2,1)}, u32[]{:S(2)}) copy-start(bf16[16,8,3,3,3]{0,1,4,3,2:T(8,128)(2,1)} %param.12) | copy-start | bytes 20740
  259.0 20.3 %copy-start.7 = (pred[8,9]{0,1:T(8,128)(4,1)S(1)}, pred[8,9]{0,1:T(8,128)(4,1)}, u32[]{:S(2)}) copy-start(pred[8,9]{0,1:T(8,128)(4,1)} %constant.40) | copy-start | bytes 220
  291.0 1.0 copy-start.3
where the time goes:
time: 297 us; the launch traced here: 293 us
  local copies, waits for them, and re-layouts  131 us (44%)
  matrix products  86 us (29%)
  starting transfers between devices  38.6 us (13%)
  waiting for transfers between devices  19 us (6%)
  blocking collectives  10.6 us (4%)
  other arithmetic  7.4 us (2%)
    conv_general_dilated x40, local copies, waits for them, and re-layouts, conv_layer(): lax.conv_general_dilated(section[None], kernel, (1, 1, 1), ((0, 0), (0, 0...  101 us
    conv_general_dilated x8, matrix products, conv_layer(): lax.conv_general_dilated(section[None], kernel, (1, 1, 1), ((0, 0), (0, 0...  74.6 us
    conv_general_dilated x5, local copies, waits for them, and re-layouts, body(): lax.conv_general_dilated(extended[None], kernel_three, (2, 2, 2), ((0, 0)...  26.5 us
    ppermute x4, starting transfers between devices, extended_2(): lax.ppermute(head, axis, [((i + 1) % count, i) for i in range(ends)])  18.3 us
    ppermute x4, starting transfers between devices, extended_2(): lax.ppermute(tail, axis, [(i, (i + 1) % count) for i in range(ends)])  15.1 us
    ppermute x2, waiting for transfers between devices, from_behind(): return lax.ppermute(shard, axis, pairs)  11.4 us
    conv_general_dilated x1, matrix products, body(): lax.conv_general_dilated(extended[None], kernel_three, (2, 2, 2), ((0, 0)...  11.3 us
    all_to_all x1, blocking collectives, body(): lax.all_to_all(sky_cube.astype(jnp.bfloat16), 'tile', split_axis=1, conca...  10.6 us
  transfers between devices with their start and end apart: 10, of which 6 were waited for; matrix products, arithmetic and copies ran while one was open for 10% of the time, Pallas kernels for 0%

commit v1 on v0

v1 whole, which is shorter than its diff:
```python
import functools

import jax
import jax.numpy as jnp
from jax import lax
from jax.experimental import pallas as pl
from jax.experimental.pallas import tpu as pltpu
from jax.sharding import PartitionSpec as P

MESH = pl.DeviceIdType.MESH
BF = jnp.bfloat16
F32 = jnp.float32

SPAN = 16
PLANES = SPAN + 5
ROWS = 24
F1, Y1 = SPAN + 3, SPAN + 3
F2, Y2 = SPAN + 1, SPAN + 1
K1 = 80
K2 = 464
K3 = 416


def iota(shape, dim):
    return lax.broadcasted_iota(jnp.int32, shape, dim)


def exchange_kernel(sky, out, raw, moved, slab, in_sem, send_sem, recv_sem):
    groups, strips = lax.axis_size("freq"), lax.axis_size("tile")
    g, t = lax.axis_index("freq"), lax.axis_index("tile")
    height = raw.shape[0]

    load = pltpu.make_async_copy(sky.at[0], raw, in_sem)
    load.start()

    barrier = pltpu.get_barrier_semaphore()

    def greet(group, strip):
        pl.semaphore_signal(barrier, inc=1, device_id=(group, strip), device_id_type=MESH)

    @pl.loop(1, strips)
    def _(k):
        greet(g, lax.rem(t + k, strips))

    @pl.when(g < groups - 1)
    def _():
        for strip in (0, 1):
            greet(g + 1, strip)

    @pl.when(g > 0)
    def _():
        for strip in (strips - 3, strips - 2, strips - 1):
            greet(g - 1, strip)

    lane = iota((128, 128), 1)
    column = jnp.where(lane < 64, 2 * lane, 2 * lane - 127)
    order = (iota((128, 128), 0) == column).astype(F32).astype(BF)
    load.wait()
    values = jnp.dot(raw[...].astype(BF), order, preferred_element_type=F32)
    moved[0:8, :] = jnp.zeros((8, 128), F32)
    moved[height : height + 16, :] = jnp.zeros((16, 128), F32)
    moved[4 : height + 4, :] = values
    slab[...] = moved[...].reshape(slab.shape).astype(BF)

    upper = t >= strips - 3
    low = t < 2
    beyond = jnp.logical_or(jnp.logical_and(low, g > 0), jnp.logical_and(upper, g < groups - 1))
    other = jnp.where(low, jnp.maximum(g - 1, 0), jnp.minimum(g + 1, groups - 1))
    plane = 3 + t
    far_plane = jnp.where(low, SPAN + 3 + t, jnp.maximum(t - (strips - 3), 0))

    @pl.when(beyond)
    def _():
        pl.semaphore_wait(barrier, 2 * strips - 1)

    @pl.when(jnp.logical_not(beyond))
    def _():
        pl.semaphore_wait(barrier, strips - 1)

    def near(k):
        strip = lax.rem(t + k, strips)
        return pltpu.make_async_remote_copy(
            src_ref=slab.at[pl.ds(2 * strip, 3)],
            dst_ref=out.at[plane],
            send_sem=send_sem.at[k],
            recv_sem=recv_sem.at[plane],
            device_id=(g, strip),
            device_id_type=MESH,
        )

    def far(k):
        strip = lax.rem(t + k, strips)
        return pltpu.make_async_remote_copy(
            src_ref=slab.at[pl.ds(2 * strip, 3)],
            dst_ref=out.at[far_plane],
            send_sem=send_sem.at[strips + k],
            recv_sem=recv_sem.at[far_plane],
            device_id=(other, strip),
            device_id_type=MESH,
        )

    @pl.when(beyond)
    def _():
        @pl.loop(0, strips)
        def _(k):
            far(k).start()

    @pl.loop(1, strips)
    def _(k):
        near(k).start()

    out[plane] = slab[pl.ds(2 * t, 3)]

    def arrived(p):
        pltpu.make_async_copy(out.at[p], out.at[p], recv_sem.at[p]).wait()

    @pl.loop(1, strips)
    def _(k):
        arrived(3 + lax.rem(t + k, strips))

    @pl.when(g > 0)
    def _():
        for p in range(3):
            arrived(p)

    @pl.when(g == 0)
    def _():
        out[0:3] = jnp.zeros((3, 3, 8, 128), BF)

    @pl.when(g < groups - 1)
    def _():
        for p in (SPAN + 3, SPAN + 4):
            arrived(p)

    @pl.when(g == groups - 1)
    def _():
        out[SPAN + 3 : SPAN + 5] = jnp.zeros((2, 3, 8, 128), BF)

    @pl.loop(1, strips)
    def _(k):
        near(k).wait_send()

    @pl.when(beyond)
    def _():
        @pl.loop(0, strips)
        def _(k):
            far(k).wait_send()


def exchange(sky_cube):
    height = sky_cube.shape[1]
    strips = height // SPAN
    return pl.pallas_call(
        exchange_kernel,
        out_shape=jax.ShapeDtypeStruct((PLANES, 3, 8, 128), BF),
        in_specs=[pl.BlockSpec(memory_space=pl.ANY)],
        out_specs=pl.BlockSpec(memory_space=pltpu.VMEM),
        scratch_shapes=[
            pltpu.VMEM((height, 128), F32),
            pltpu.VMEM((height + 16, 128), F32),
            pltpu.VMEM(((height + 16) // 8, 8, 128), BF),
            pltpu.SemaphoreType.DMA,
            pltpu.SemaphoreType.DMA((2 * strips,)),
            pltpu.SemaphoreType.DMA((PLANES,)),
        ],
        compiler_params=pltpu.CompilerParams(
            collective_id=0, has_side_effects=True, vmem_limit_bytes=8 << 20
        ),
        name="exchange",
    )(sky_cube)


def leaky(values):
    return jnp.maximum(values, 0.1 * values)


def parts_of(k):
    i = (k * 2428) >> 16
    k = k - 27 * i
    a = (k * 7282) >> 16
    k = k - 9 * a
    b = (k * 21846) >> 16
    return i, a, b, k - 3 * b


def placed(flat, columns, target):
    k = flat.shape[1]
    source = iota((k, columns), 0)
    hits = iota((k, columns), 1) == target(*parts_of(source))
    return jnp.dot(flat, hits.astype(F32).astype(BF), preferred_element_type=F32)


def beside(values):
    lane = iota(values.shape, 1)
    swapped = pltpu.roll(values, 64, 1)
    before = jnp.where(lane < 64, pltpu.roll(values, 65, 1), swapped)
    after = jnp.where(lane < 64, swapped, pltpu.roll(values, 63, 1))
    return (
        jnp.where(lane == 0, 0.0, before),
        values,
        jnp.where(lane == 127, 0.0, after),
    )


def column_of(bias, rows, count):
    row = iota((count, 128), 0)
    block = jnp.zeros((count, 128), F32)
    for o in range(count):
        block = jnp.where(row == o, bias[o], block)
    return jnp.concatenate([block] * (rows // count), axis=0)


def banded_weights(k1, k2, k3, w1, w2, w3):
    base = placed(k1[...], 256, lambda i, a, b, c: jnp.where(i == 0, a * K1 + c * ROWS + 1 + b, -1))
    for y in range(0, Y1, 2):
        both = [pltpu.roll(base, s, 1) if s else base for s in (y, y + 1)]
        w1[8 * y : 8 * y + 16, :] = jnp.concatenate(both, axis=0).astype(BF)

    base = placed(
        k2[...], 1408, lambda i, a, b, c: jnp.where(i < 8, a * K2 + c * (8 * Y1) + 8 * b + i, -1)
    )
    for y in range(0, Y2, 2):
        both = [pltpu.roll(base, 8 * s, 1) if s else base for s in (y, min(y + 1, Y2 - 1))]
        w2[8 * y : 8 * y + 16, :] = jnp.concatenate(both, axis=0).astype(BF)

    base = placed(
        k3[...], 1280, lambda i, a, b, c: jnp.where(i < 8, a * K3 + c * (8 * Y2) + 8 * b + i, -1)
    )
    rows = [pltpu.roll(base, 16 * y, 1) if y else base for y in range(SPAN // 2)]
    by_row = jnp.concatenate(rows, axis=0).astype(BF)
    r = iota((128, 128), 0)
    swap = iota((128, 128), 1) == (r & 7) * 16 + (r >> 3)
    w3[...] = jnp.dot(
        swap.astype(F32).astype(BF), by_row, preferred_element_type=F32
    ).astype(BF)


def conv_kernel(pos, cube, k1, k2, k3, b1, b2, b3, out, x1, x2, l2, x3, w1, w2, w3):
    if pos is None:
        groups, strips = lax.axis_size("freq"), lax.axis_size("tile")
        g, t = lax.axis_index("freq"), lax.axis_index("tile")
    else:
        groups, strips, g, t = pos
    banded_weights(k1, k2, k3, w1, w2, w3)

    def one_if(inside):
        return jnp.where(inside, 1.0, 0.0).astype(F32)

    for f in range(PLANES):
        pieces = beside(cube[f].astype(F32))
        block = jnp.concatenate([*pieces, jnp.zeros((K1 - 3 * ROWS, 128), F32)], axis=0)
        x1[f * K1 : (f + 1) * K1, :] = block.astype(BF)

    first_g, last_g = one_if(g > 0), one_if(g < groups - 1)
    first_t, last_t = one_if(t > 0), one_if(t < strips - 1)
    bias = column_of(b1, 8 * Y1, 8)
    row = iota((8 * Y1, 128), 0)
    keep = jnp.where(row < 16, first_t, jnp.where(row >= 8 * (Y1 - 1), last_t, 1.0))
    weights = w1[0 : 8 * Y1, 0 : 3 * K1]
    for f in range(0, F1, 2):
        fs = [f, f + 1] if f + 1 < F1 else [f]
        data = jnp.concatenate([x1[h * K1 : (h + 3) * K1, :] for h in fs], axis=1)
        sums = jnp.dot(weights, data, preferred_element_type=F32)
        for n, h in enumerate(fs):
            values = leaky(sums[:, 128 * n : 128 * (n + 1)] + bias) * keep
            if h < 2:
                values = values * first_g
            if h == F1 - 1:
                values = values * last_g
            block = jnp.concatenate(
                [*beside(values), jnp.zeros((K2 - 24 * Y1, 128), F32)], axis=0
            )
            x2[h * K2 : (h + 1) * K2, :] = block.astype(BF)

    bias = column_of(b2, 8 * Y2, 8)
    keep = jnp.where(iota((8 * Y2, 128), 0) < 8, first_t, 1.0)
    weights = w2[0 : 8 * Y2, 0 : 3 * K2]
    for f in range(0, F2, 2):
        fs = [f, f + 1] if f + 1 < F2 else [f]
        data = jnp.concatenate([x2[h * K2 : (h + 3) * K2, :] for h in fs], axis=1)
        sums = jnp.dot(weights, data, preferred_element_type=F32)
        for n, h in enumerate(fs):
            values = leaky(sums[:, 128 * n : 128 * (n + 1)] + bias) * keep
            if h == 0:
                values = values * first_g
            l2[h] = values

    half = SPAN // 2
    lane = iota((8 * Y2, 128), 1)
    for f in range(half + 1):
        lower, upper = l2[f], l2[f + half]
        before = jnp.where(lane < 64, pltpu.roll(lower, 65, 1), pltpu.roll(upper, 1, 1))
        block = jnp.concatenate(
            [
                jnp.where((lane & 63) == 0, 0.0, before),
                jnp.where(lane < 64, lower, pltpu.roll(upper, 64, 1)),
                jnp.where(lane < 64, pltpu.roll(lower, 64, 1), upper),
                jnp.zeros((K3 - 24 * Y2, 128), F32),
            ],
            axis=0,
        )
        x3[f * K3 : (f + 1) * K3, :] = block.astype(BF)
    bias = jnp.concatenate([jnp.full((8, 128), b3[o], F32) for o in range(16)], axis=0)
    weights = w3[:, 0 : 3 * K3]
    quarter = half // 2
    for f in range(0, quarter, 2):
        data = jnp.concatenate(
            [x3[2 * h * K3 : (2 * h + 3) * K3, :] for h in (f, f + 1)], axis=1
        )
        sums = jnp.dot(weights, data, preferred_element_type=F32)
        for n, h in enumerate((f, f + 1)):
            values = leaky(sums[:, 128 * n : 128 * (n + 1)] + bias)
            out[:, h, :, :] = values[:, 0:64].reshape(16, 8, 64).astype(BF)
            swapped = pltpu.roll(values, 64, 1)
            out[:, h + quarter, :, :] = swapped[:, 0:64].reshape(16, 8, 64).astype(BF)


def convolutions(cube, k1, k2, k3, b1, b2, b3, pos=None, interpret=False):
    vmem = pl.BlockSpec(memory_space=pltpu.VMEM)
    smem = pl.BlockSpec(memory_space=pltpu.SMEM)
    half = SPAN // 2
    return pl.pallas_call(
        functools.partial(conv_kernel, pos),
        out_shape=jax.ShapeDtypeStruct((16, half, half, 64), BF),
        in_specs=[vmem, vmem, vmem, vmem, smem, smem, smem],
        out_specs=vmem,
        scratch_shapes=[
            pltpu.VMEM((PLANES * K1, 128), BF),
            pltpu.VMEM((F1 * K2, 128), BF),
            pltpu.VMEM((F2, 8 * Y2, 128), F32),
            pltpu.VMEM(((half + 1) * K3, 128), BF),
            pltpu.VMEM((160, 256), BF),
            pltpu.VMEM((144, 1408), BF),
            pltpu.VMEM((128, 1280), BF),
        ],
        compiler_params=pltpu.CompilerParams(vmem_limit_bytes=24 << 20),
        interpret=interpret,
        name="convolutions",
    )(cube, k1, k2, k3, b1, b2, b3)


def flat(kernel):
    rows = kernel.shape[0]
    count = kernel.size // rows
    return jnp.pad(kernel.reshape(rows, count), ((0, 0), (0, -count % 128)))


def body(sky_cube, kernel_one, bias_one, kernel_two, bias_two, kernel_three, bias_three):
    cube = exchange(sky_cube).reshape(PLANES, ROWS, 128)
    return convolutions(
        cube,
        flat(kernel_one),
        flat(kernel_two),
        flat(kernel_three),
        bias_one,
        bias_two,
        bias_three,
    )


def solution(mesh):
    return jax.shard_map(
        body,
        mesh=mesh,
        in_specs=(P(("freq", "tile"), None, None), P(), P(), P(), P(), P(), P()),
        out_specs=P(None, "freq", "tile", None),
        check_vma=False,
    )
```

time: 297 us -> 22.2 us (0.07)
  the two profiles are of different devices: /device:TPU:34 before, /device:TPU:39 now
where the time goes in v1:
time: 22.2 us; the launch traced here: 21.9 us
  Pallas kernels  17.7 us (80%)
  local copies, waits for them, and re-layouts  4.17 us (19%)
    pallas_call x1, Pallas kernels, exchange(): pl.pallas_call(exchange_kernel, out_shape=jax.ShapeDtypeStruct((PLANES, 3...  13.7 us
    pallas_call x1, Pallas kernels, convolutions(): pl.pallas_call(functools.partial(conv_kernel, pos), out_shape=jax.ShapeDt...  3.94 us
    unnamed x12, local copies, waits for them, and re-layouts  3.12 us
    reshape x6, local copies, waits for them, and re-layouts, flat(): return jnp.pad(kernel.reshape(rows, count), ((0, 0), (0, -count % 128)))  1.03 us

profile of v1, /device:TPU:39, one launch (start us, length us, event | category | flops | bytes accessed | tf_op | source)
XLA Modules:
  0.0 21.9 jit_solution(8280658868649113219)
XLA Ops:
  0.0 0.7 %reshape.13 = bf16[8,27]{0,1:T(8,128)(2,1)S(1)} reshape(bf16[8,1,3,3,3]{0,4,3,2,1:T(4,128)(2,1)} %param.8) | data formatting | bytes 864 | tf_op jit(solution)/shard_map/reshape | solution.py:345
  0.7 0.1 copy.11
  0.8 0.9 %copy.12 = bf16[8,8,3,3,3]{0,4,3,2,1:T(4,128)(2,1)S(1)} copy(bf16[8,8,3,3,3]{1,0,4,3,2:T(8,128)(2,1)} %param.10) | data formatting | bytes 6912 | tf_op args[3]
  1.8 0.0 copy-start.4
  1.8 0.1 copy.13
  1.9 0.7 %copy-done.4 = bf16[16,8,3,3,3]{0,1,4,3,2:T(8,128)(2,1)S(1)} copy-done((bf16[16,8,3,3,3]{0,1,4,3,2:T(8,128)(2,1)S(1)}, bf16[16,8,3,3,3]{0,1,4,3,2:T(8,128)(2,1)}, u32[]{:S(2)}) %copy-start.4) | copy-done | bytes 6936
  2.6 0.0 copy-start
  2.7 0.1 copy.15
  2.8 0.8 %copy-done = f32[1,256,128]{2,1,0:T(8,128)S(1)} copy-done((f32[1,256,128]{2,1,0:T(8,128)S(1)}, f32[1,256,128]{2,1,0:T(8,128)}, u32[]{:S(2)}) %copy-start) | copy-done | bytes 131096
  3.6 13.7 %exchange.1 = bf16[21,3,8,128]{3,2,1,0:T(8,128)(2,1)S(1)} custom-call(f32[1,256,128]{2,1,0:T(8,128)S(1)} %copy-done), custom_call_target="tpu_custom_call" | custom-call | tf_op jit(solution)/shard_map/exchange/pallas_call | solution.py:153
  17.3 0.0 copy-start.1
  17.3 0.0 copy-start.2
  17.3 0.0 copy-start.3
  17.3 0.6 %copy-done.1 = f32[8]{0:T(128)S(1)} copy-done((f32[8]{0:T(128)S(1)}, f32[8]{0:T(128)}, u32[]{:S(2)}) %copy-start.1) | copy-done | bytes 56
  17.9 0.0 copy-done.2
  18.0 0.0 copy-done.3
  18.0 3.9 %convolutions.1 = bf16[16,8,8,64]{3,2,1,0:T(8,128)(2,1)} custom-call(bf16[21,24,128]{2,1,0:T(8,128)(2,1)S(1)} %bitcast.7, bf16[8,128]{1,0:T(8,128)(2,1)S(1)} %pad.12.k1, bf16[8,256]{1,0:T(8,128)(2,1)S(1)} %pad.13.k2, bf16[16,256]{1,0:T(8,128)(2,1)S(1)} %pad.14.k3, f32[8]{0:T(128)S(1)} %copy-done.1, f32[8]{0:T(128)S(1)} %copy-done.2, f32[16]{0:T(128)S(1)} %copy-done.3), custom_call_target="tpu_custom_call" | custom-call | tf_op jit(solution)/shard_map/convolutions/pallas_call | solution.py:322
  (6 shorter events, 0.1 us)
Async XLA Ops:
  1.8 0.8 %copy-start.4 = (bf16[16,8,3,3,3]{0,1,4,3,2:T(8,128)(2,1)S(1)}, bf16[16,8,3,3,3]{0,1,4,3,2:T(8,128)(2,1)}, u32[]{:S(2)}) copy-start(bf16[16,8,3,3,3]{0,1,4,3,2:T(8,128)(2,1)} %param.12) | copy-start | bytes 20740
  2.6 0.9 %copy-start = (f32[1,256,128]{2,1,0:T(8,128)S(1)}, f32[1,256,128]{2,1,0:T(8,128)}, u32[]{:S(2)}) copy-start(f32[1,256,128]{2,1,0:T(8,128)} %sky.1) | copy-start | bytes 393220
  17.3 0.7 %copy-start.1 = (f32[8]{0:T(128)S(1)}, f32[8]{0:T(128)}, u32[]{:S(2)}) copy-start(f32[8]{0:T(128)} %b1.1) | copy-start | bytes 100
  17.3 0.7 %copy-start.2 = (f32[8]{0:T(128)S(1)}, f32[8]{0:T(128)}, u32[]{:S(2)}) copy-start(f32[8]{0:T(128)} %b2.1) | copy-start | bytes 100
  17.3 0.7 %copy-start.3 = (f32[16]{0:T(128)S(1)}, f32[16]{0:T(128)}, u32[]{:S(2)}) copy-start(f32[16]{0:T(128)} %b3.1) | copy-start | bytes 196

commit v2 on v0

v2 whole, which is shorter than its diff:
```python
import jax
import jax.numpy as jnp
from jax import lax
from jax.experimental import pallas as pl
from jax.experimental.pallas import tpu as pltpu
from jax.sharding import PartitionSpec as P

MESH = pl.DeviceIdType.MESH
BF = jnp.bfloat16
F32 = jnp.float32

SPAN = 16
PLANES = SPAN + 5
ROWS = 24
F1, Y1 = SPAN + 3, SPAN + 3
F2, Y2 = SPAN + 1, SPAN + 1
K1 = 80
K2 = 464
K3 = 416


def iota(shape, dim):
    return lax.broadcasted_iota(jnp.int32, shape, dim)


def leaky(values):
    return jnp.maximum(values, 0.1 * values)


def beside(values):
    lane = iota(values.shape, 1)
    swapped = pltpu.roll(values, 64, 1)
    before = jnp.where(lane < 64, pltpu.roll(values, 65, 1), swapped)
    after = jnp.where(lane < 64, swapped, pltpu.roll(values, 63, 1))
    return (
        jnp.where(lane == 0, 0.0, before),
        values,
        jnp.where(lane == 127, 0.0, after),
    )


def column_of(bias, rows, count):
    row = iota((count, 128), 0)
    block = jnp.zeros((count, 128), F32)
    for o in range(count):
        block = jnp.where(row == o, bias[o], block)
    return jnp.concatenate([block] * (rows // count), axis=0)


def taps():
    return [(a, b, c) for a in range(3) for b in range(3) for c in range(3)]


def one_if(inside):
    return jnp.where(inside, 1.0, 0.0).astype(F32)


def banded_weights(k1, k2, k3, stack1, base2, stack3, w1, w2, w3):
    stack1[...] = jnp.zeros(stack1.shape, F32)
    for a in range(3):
        for b in range(3):
            at = 8 * (3 * a + b)
            stack1[at : at + 3, 0:8] = k1[0, a, b].astype(F32)
    source = iota((128, 256), 0)
    tap, c = source >> 3, source & 7
    a = (tap * 21846) >> 16
    target = jnp.where((tap < 9) & (c < 3), a * K1 + c * ROWS + 1 + tap - 3 * a, -1)
    base = jnp.dot(
        stack1[...].T[0:8].astype(BF),
        (iota((128, 256), 1) == target).astype(F32).astype(BF),
        preferred_element_type=F32,
    )
    for y in range(0, Y1, 2):
        both = [pltpu.roll(base, s, 1) if s else base for s in (y, y + 1)]
        w1[8 * y : 8 * y + 16, :] = jnp.concatenate(both, axis=0).astype(BF)

    base2[...] = jnp.zeros(base2.shape, F32)
    for a, b, c in taps():
        at = a * K2 + c * (8 * Y1) + 8 * b
        base2[:, at : at + 8] = k2[a, b, c].astype(F32)
    base = base2[...]
    for y in range(0, Y2, 2):
        both = [pltpu.roll(base, 8 * s, 1) if s else base for s in (y, min(y + 1, Y2 - 1))]
        w2[8 * y : 8 * y + 16, :] = jnp.concatenate(both, axis=0).astype(BF)

    stack3[...] = jnp.zeros(stack3.shape, F32)
    for n, (a, b, c) in enumerate(taps()):
        stack3[8 * n : 8 * n + 8, 0:16] = k3[a, b, c].astype(F32)
    source = iota((256, 1280), 0)
    tap, i = source >> 3, source & 7
    a = (tap * 7282) >> 16
    rest = tap - 9 * a
    b = (rest * 21846) >> 16
    target = jnp.where(tap < 27, a * K3 + (rest - 3 * b) * (8 * Y2) + 8 * b + i, -1)
    base = jnp.dot(
        stack3[...].T[0:16].astype(BF),
        (iota((256, 1280), 1) == target).astype(F32).astype(BF),
        preferred_element_type=F32,
    )
    rows = [pltpu.roll(base, 16 * y, 1) if y else base for y in range(SPAN // 2)]
    by_row = jnp.concatenate(rows, axis=0).astype(BF)
    r = iota((128, 128), 0)
    swap = iota((128, 128), 1) == (r & 7) * 16 + (r >> 3)
    w3[...] = jnp.dot(
        swap.astype(F32).astype(BF), by_row, preferred_element_type=F32
    ).astype(BF)


def two_layers(place, cube, far_channels, b1, b2, x1, x2, l2, x3, w1, w2):
    groups, strips, g, t = place
    first_g, last_g = one_if(g > 0), one_if(g < groups - 1)
    first_t, last_t = one_if(t > 0), one_if(t < strips - 1)

    def operand(f):
        pieces = beside(cube[f].reshape(ROWS, 128).astype(F32))
        block = jnp.concatenate([*pieces, jnp.zeros((K1 - 3 * ROWS, 128), F32)], axis=0)
        x1[f * K1 : (f + 1) * K1, :] = block.astype(BF)

    bias1 = column_of(b1, 8 * Y1, 8)
    row = iota((8 * Y1, 128), 0)
    keep1 = jnp.where(row < 16, first_t, jnp.where(row >= 8 * (Y1 - 1), last_t, 1.0))

    def layer_one(*fs):
        data = jnp.concatenate([x1[h * K1 : (h + 3) * K1, :] for h in fs], axis=1)
        sums = jnp.dot(w1[0 : 8 * Y1, 0 : 3 * K1], data, preferred_element_type=F32)
        for n, h in enumerate(fs):
            values = leaky(sums[:, 128 * n : 128 * (n + 1)] + bias1) * keep1
            if h < 2:
                values = values * first_g
            if h == F1 - 1:
                values = values * last_g
            block = jnp.concatenate(
                [*beside(values), jnp.zeros((K2 - 24 * Y1, 128), F32)], axis=0
            )
            x2[h * K2 : (h + 1) * K2, :] = block.astype(BF)

    bias2 = column_of(b2, 8 * Y2, 8)
    keep2 = jnp.where(iota((8 * Y2, 128), 0) < 8, first_t, 1.0)

    def layer_two(*fs):
        data = jnp.concatenate([x2[h * K2 : (h + 3) * K2, :] for h in fs], axis=1)
        sums = jnp.dot(w2[0 : 8 * Y2, 0 : 3 * K2], data, preferred_element_type=F32)
        for n, h in enumerate(fs):
            values = leaky(sums[:, 128 * n : 128 * (n + 1)] + bias2) * keep2
            if h == 0:
                values = values * first_g
            l2[h] = values

    half = SPAN // 2
    lane = iota((8 * Y2, 128), 1)

    def joined(f):
        lower, upper = l2[f], l2[f + half]
        before = jnp.where(lane < 64, pltpu.roll(lower, 65, 1), pltpu.roll(upper, 1, 1))
        block = jnp.concatenate(
            [
                jnp.where((lane & 63) == 0, 0.0, before),
                jnp.where(lane < 64, lower, pltpu.roll(upper, 64, 1)),
                jnp.where(lane < 64, pltpu.roll(lower, 64, 1), upper),
                jnp.zeros((K3 - 24 * Y2, 128), F32),
            ],
            axis=0,
        )
        x3[f * K3 : (f + 1) * K3, :] = block.astype(BF)

    for f in range(3, SPAN + 3):
        operand(f)
    for f in range(3, SPAN + 1, 2):
        layer_one(f, f + 1)
    for f in range(3, SPAN - 1, 2):
        layer_two(f, f + 1)
    for f in range(3, 7):
        joined(f)
    far_channels()
    for f in (0, 1, 2, SPAN + 3, SPAN + 4):
        operand(f)
    layer_one(0, 1)
    layer_one(2, 17)
    layer_one(18)
    layer_two(0, 1)
    layer_two(2, 15)
    layer_two(16)
    for f in (0, 1, 2, 7, 8):
        joined(f)


def spread_kernel(
    sky, k1_in, k2_in, k3_in, b1_in, b2_in, b3_in,
    x3, w3, bias3,
    raw, moved, slab, cube, k1, k2, k3, b1, b2, b3, stack1, base2, stack3, w1, w2, x1, x2, l2,
    in_sem, send_sem, recv_sem,
):
    groups, strips = lax.axis_size("freq"), lax.axis_size("tile")
    g, t = lax.axis_index("freq"), lax.axis_index("tile")
    height = raw.shape[0]

    barrier = pltpu.get_barrier_semaphore()

    def greet(group, strip):
        pl.semaphore_signal(barrier, inc=1, device_id=(group, strip), device_id_type=MESH)

    @pl.when(g < groups - 1)
    def _():
        for strip in (0, 1):
            greet(g + 1, strip)

    @pl.when(g > 0)
    def _():
        for strip in (strips - 3, strips - 2, strips - 1):
            greet(g - 1, strip)

    @pl.loop(1, strips)
    def _(k):
        greet(g, lax.rem(t + k, strips))

    pairs = [(sky.at[0], raw), (k1_in, k1), (k2_in, k2), (k3_in, k3), (b1_in, b1), (b2_in, b2), (b3_in, b3)]
    loads = [pltpu.make_async_copy(a, b, in_sem.at[n]) for n, (a, b) in enumerate(pairs)]
    for load in loads:
        load.start()

    lane = iota((128, 128), 1)
    column = jnp.where(lane < 64, 2 * lane, 2 * lane - 127)
    order = (iota((128, 128), 0) == column).astype(F32).astype(BF)
    moved[0:8, :] = jnp.zeros((8, 128), F32)
    moved[height : height + 16, :] = jnp.zeros((16, 128), F32)
    loads[0].wait()
    values = jnp.dot(raw[...].astype(BF), order, preferred_element_type=F32)
    moved[4 : height + 4, :] = values
    slab[...] = moved[...].reshape(slab.shape).astype(BF)

    upper = t >= strips - 3
    low = t < 2
    beyond = jnp.logical_or(jnp.logical_and(low, g > 0), jnp.logical_and(upper, g < groups - 1))
    other = jnp.where(low, jnp.maximum(g - 1, 0), jnp.minimum(g + 1, groups - 1))
    plane = 3 + t
    far_plane = jnp.where(low, SPAN + 3 + t, jnp.maximum(t - (strips - 3), 0))

    @pl.when(beyond)
    def _():
        pl.semaphore_wait(barrier, 2 * strips - 1)

    @pl.when(jnp.logical_not(beyond))
    def _():
        pl.semaphore_wait(barrier, strips - 1)

    def near(k):
        strip = lax.rem(t + k, strips)
        return pltpu.make_async_remote_copy(
            src_ref=slab.at[pl.ds(2 * strip, 3)],
            dst_ref=cube.at[plane],
            send_sem=send_sem.at[k],
            recv_sem=recv_sem.at[plane],
            device_id=(g, strip),
            device_id_type=MESH,
        )

    def far(k):
        strip = lax.rem(t + k, strips)
        return pltpu.make_async_remote_copy(
            src_ref=slab.at[pl.ds(2 * strip, 3)],
            dst_ref=cube.at[far_plane],
            send_sem=send_sem.at[strips + k],
            recv_sem=recv_sem.at[far_plane],
            device_id=(other, strip),
            device_id_type=MESH,
        )

    @pl.when(beyond)
    def _():
        @pl.loop(0, strips)
        def _(k):
            far(k).start()

    @pl.loop(1, strips)
    def _(k):
        near(k).start()

    cube[plane] = slab[pl.ds(2 * t, 3)]

    for load in loads[1:]:
        load.wait()
    banded_weights(k1, k2, k3, stack1, base2, stack3, w1, w2, w3)
    for o in range(16):
        bias3[8 * o : 8 * o + 8, :] = jnp.full((8, 128), b3[o], F32)

    def arrived(p):
        pltpu.make_async_copy(cube.at[p], cube.at[p], recv_sem.at[p]).wait()

    @pl.loop(1, strips)
    def _(k):
        arrived(3 + lax.rem(t + k, strips))

    def far_channels():
        @pl.when(g > 0)
        def _():
            for p in range(3):
                arrived(p)

        @pl.when(g == 0)
        def _():
            cube[0:3] = jnp.zeros((3, 3, 8, 128), BF)

        @pl.when(g < groups - 1)
        def _():
            for p in (SPAN + 3, SPAN + 4):
                arrived(p)

        @pl.when(g == groups - 1)
        def _():
            cube[SPAN + 3 : SPAN + 5] = jnp.zeros((2, 3, 8, 128), BF)

    two_layers((groups, strips, g, t), cube, far_channels, b1, b2, x1, x2, l2, x3, w1, w2)

    @pl.loop(1, strips)
    def _(k):
        near(k).wait_send()

    @pl.when(beyond)
    def _():
        @pl.loop(0, strips)
        def _(k):
            far(k).wait_send()


X3_SHAPE = ((SPAN // 2 + 1) * K3, 128)
WEIGHT_SCRATCH = [
    pltpu.VMEM((128, 128), F32),
    pltpu.VMEM((8, 1408), F32),
    pltpu.VMEM((256, 128), F32),
    pltpu.VMEM((160, 256), BF),
    pltpu.VMEM((144, 1408), BF),
]
LAYER_SCRATCH = [
    pltpu.VMEM((PLANES * K1, 128), BF),
    pltpu.VMEM((F1 * K2, 128), BF),
    pltpu.VMEM((F2, 8 * Y2, 128), F32),
]


def first_layers(sky_cube, k1, k2, k3, b1, b2, b3):
    height = sky_cube.shape[1]
    strips = height // SPAN
    operands = [
        pltpu.with_memory_space_constraint(x, pltpu.HBM)
        for x in (sky_cube, k1, k2, k3, b1, b2, b3)
    ]
    vmem = pl.BlockSpec(memory_space=pltpu.VMEM)
    return pl.pallas_call(
        spread_kernel,
        out_shape=[
            jax.ShapeDtypeStruct(X3_SHAPE, BF),
            jax.ShapeDtypeStruct((128, 1280), BF),
            jax.ShapeDtypeStruct((128, 128), F32),
        ],
        in_specs=[pl.BlockSpec(memory_space=pltpu.HBM)] * len(operands),
        out_specs=[vmem] * 3,
        scratch_shapes=[
            pltpu.VMEM((height, 128), F32),
            pltpu.VMEM((height + 16, 128), F32),
            pltpu.VMEM(((height + 16) // 8, 8, 128), BF),
            pltpu.VMEM((PLANES, 3, 8, 128), BF),
            pltpu.VMEM(k1.shape, BF),
            pltpu.VMEM(k2.shape, BF),
            pltpu.VMEM(k3.shape, BF),
            pltpu.SMEM(b1.shape, F32),
            pltpu.SMEM(b2.shape, F32),
            pltpu.SMEM(b3.shape, F32),
            *WEIGHT_SCRATCH,
            *LAYER_SCRATCH,
            pltpu.SemaphoreType.DMA((len(operands),)),
            pltpu.SemaphoreType.DMA((2 * strips,)),
            pltpu.SemaphoreType.DMA((PLANES,)),
        ],
        compiler_params=pltpu.CompilerParams(
            collective_id=0, has_side_effects=True, vmem_limit_bytes=24 << 20
        ),
        name="first_layers",
    )(*operands)


def third_kernel(x3, w3, bias3, out):
    quarter = SPAN // 4
    for f in range(0, quarter, 2):
        data = jnp.concatenate(
            [x3[2 * h * K3 : (2 * h + 3) * K3, :] for h in (f, f + 1)], axis=1
        )
        sums = jnp.dot(w3[:, 0 : 3 * K3], data, preferred_element_type=F32)
        for n, h in enumerate((f, f + 1)):
            values = leaky(sums[:, 128 * n : 128 * (n + 1)] + bias3[...])
            out[:, h, :, :] = values[:, 0:64].reshape(16, 8, 64).astype(BF)
            swapped = pltpu.roll(values, 64, 1)
            out[:, h + quarter, :, :] = swapped[:, 0:64].reshape(16, 8, 64).astype(BF)


def third_layer(x3, w3, bias3):
    vmem = pl.BlockSpec(memory_space=pltpu.VMEM)
    half = SPAN // 2
    return pl.pallas_call(
        third_kernel,
        out_shape=jax.ShapeDtypeStruct((16, half, half, 64), BF),
        in_specs=[vmem] * 3,
        out_specs=vmem,
        compiler_params=pltpu.CompilerParams(vmem_limit_bytes=8 << 20),
        name="third_layer",
    )(x3, w3, bias3)


def body(sky_cube, kernel_one, bias_one, kernel_two, bias_two, kernel_three, bias_three):
    return third_layer(
        *first_layers(
            sky_cube,
            kernel_one.transpose(1, 2, 3, 4, 0),
            kernel_two.transpose(2, 3, 4, 0, 1),
            kernel_three.transpose(2, 3, 4, 1, 0),
            bias_one,
            bias_two,
            bias_three,
        )
    )


def solution(mesh):
    return jax.shard_map(
        body,
        mesh=mesh,
        in_specs=(P(("freq", "tile"), None, None), P(), P(), P(), P(), P(), P()),
        out_specs=P(None, "freq", "tile", None),
        check_vma=False,
    )
```

time: 297 us -> 16.1 us (0.05)
  the two profiles are of different devices: /device:TPU:34 before, /device:TPU:15 now
where the time goes in v2:
time: 16.1 us; the launch traced here: 16 us
  Pallas kernels  16 us (99%)
    pallas_call x1, Pallas kernels, first_layers(): pl.pallas_call(spread_kernel, out_shape=[jax.ShapeDtypeStruct(X3_SHAPE, B...  14.8 us
    pallas_call x1, Pallas kernels, third_layer(): pl.pallas_call(third_kernel, out_shape=jax.ShapeDtypeStruct((16, half, ha...  1.14 us

profile of v2, /device:TPU:15, one launch (start us, length us, event | category | flops | bytes accessed | tf_op | source)
XLA Modules:
  0.0 16.0 jit_solution(9040188822083289643)
XLA Ops:
  0.0 14.8 %first_layers.1 = (bf16[3744,128]{1,0:T(8,128)(2,1)S(1)}, bf16[128,1280]{1,0:T(8,128)(2,1)S(1)}, f32[128,128]{1,0:T(8,128)S(1)}) custom-call(f32[1,256,128]{2,1,0:T(8,128)} %sky.1, bf16[1,3,3,3,8]{4,3,2,1,0:T(4,128)(2,1)} %bitcast.5, bf16[3,3,3,8,8]{4,3,2,1,0:T(8,128)(2,1)} %bitcast.3, bf16[3,3,3,8,16]{4,3,2,1,0:T(8,128)(2,1)} %bitcast.4, f32[8]{0:T(128)} %b1_in.1, ...), custom_call_target="tpu_custom_call" | custom-call | tf_op jit(solution)/shard_map/first_layers/pallas_call | solution.py:348
  14.8 1.1 %third_layer.1 = bf16[16,8,8,64]{3,2,1,0:T(8,128)(2,1)} custom-call(bf16[3744,128]{1,0:T(8,128)(2,1)S(1)} %get-tuple-element.8.x3, bf16[128,1280]{1,0:T(8,128)(2,1)S(1)} %get-tuple-element.9.w3, f32[128,128]{1,0:T(8,128)S(1)} %get-tuple-element.10.bias3), custom_call_target="tpu_custom_call" | custom-call | tf_op jit(solution)/shard_map/third_layer/pallas_call | solution.py:398

commit v3 on v2

--- a/solution.py
+++ b/solution.py
@@ -106,7 +106,19 @@
     ).astype(BF)
 
 
-def two_layers(place, cube, far_channels, b1, b2, x1, x2, l2, x3, w1, w2):
+def third_matmul(x3, first, w3, bias3, out):
+    data = jnp.concatenate(
+        [x3[h * K3 : (h + 3) * K3, :] for h in (first, first + 2)], axis=1
+    )
+    sums = jnp.dot(w3[:, 0 : 3 * K3], data, preferred_element_type=F32)
+    for n in range(2):
+        values = leaky(sums[:, 128 * n : 128 * (n + 1)] + bias3[...])
+        out[:, n, :, :] = values[:, 0:64].reshape(16, 8, 64).astype(BF)
+        swapped = pltpu.roll(values, 64, 1)
+        out[:, n + 2, :, :] = swapped[:, 0:64].reshape(16, 8, 64).astype(BF)
+
+
+def all_layers(place, cube, arrive, b1, b2, bias3, x1, x2, l2, x3_upper, x3, w1, w2, w3, upper):
     groups, strips, g, t = place
     first_g, last_g = one_if(g > 0), one_if(g < groups - 1)
     first_t, last_t = one_if(t > 0), one_if(t < strips - 1)
@@ -146,11 +158,10 @@
                 values = values * first_g
             l2[h] = values
 
-    half = SPAN // 2
     lane = iota((8 * Y2, 128), 1)
 
-    def joined(f):
-        lower, upper = l2[f], l2[f + half]
+    def joined(to, at, f):
+        lower, upper = l2[f], l2[f + 4]
         before = jnp.where(lane < 64, pltpu.roll(lower, 65, 1), pltpu.roll(upper, 1, 1))
         block = jnp.concatenate(
             [
@@ -161,33 +172,42 @@
             ],
             axis=0,
         )
-        x3[f * K3 : (f + 1) * K3, :] = block.astype(BF)
-
-    for f in range(3, SPAN + 3):
+        to[at * K3 : (at + 1) * K3, :] = block.astype(BF)
+
+    arrive("inner")
+    for f in range(5, SPAN):
         operand(f)
-    for f in range(3, SPAN + 1, 2):
+    for f in (5, 7, 9, 11):
         layer_one(f, f + 1)
-    for f in range(3, SPAN - 1, 2):
+    for f in (5, 7, 9):
         layer_two(f, f + 1)
-    for f in range(3, 7):
-        joined(f)
-    far_channels()
-    for f in (0, 1, 2, SPAN + 3, SPAN + 4):
+    arrive("upper")
+    for f in range(SPAN, PLANES):
+        operand(f)
+    for f in (13, 15, 17):
+        layer_one(f, f + 1)
+    for f in (11, 13, 15):
+        layer_two(f, f + 1)
+    for n in range(5):
+        joined(x3_upper, n, 8 + n)
+    third_matmul(x3_upper, 0, w3, bias3, upper)
+    arrive("lower")
+    for f in range(5):
         operand(f)
     layer_one(0, 1)
-    layer_one(2, 17)
-    layer_one(18)
+    layer_one(2, 3)
+    layer_one(4)
     layer_two(0, 1)
-    layer_two(2, 15)
-    layer_two(16)
-    for f in (0, 1, 2, 7, 8):
-        joined(f)
+    layer_two(2, 3)
+    layer_two(4)
+    for n in range(5):
+        joined(x3, n, n)
 
 
 def spread_kernel(
     sky, k1_in, k2_in, k3_in, b1_in, b2_in, b3_in,
-    x3, w3, bias3,
-    raw, moved, slab, cube, k1, k2, k3, b1, b2, b3, stack1, base2, stack3, w1, w2, x1, x2, l2,
+    x3, w3, bias3, upper,
+    raw, moved, slab, cube, k1, k2, k3, b1, b2, b3, stack1, base2, stack3, w1, w2, x1, x2, l2, x3_upper,
     in_sem, send_sem, recv_sem,
 ):
     groups, strips = lax.axis_size("freq"), lax.axis_size("tile")
@@ -228,9 +248,9 @@
     moved[4 : height + 4, :] = values
     slab[...] = moved[...].reshape(slab.shape).astype(BF)
 
-    upper = t >= strips - 3
+    high = t >= strips - 3
     low = t < 2
-    beyond = jnp.logical_or(jnp.logical_and(low, g > 0), jnp.logical_and(upper, g < groups - 1))
+    beyond = jnp.logical_or(jnp.logical_and(low, g > 0), jnp.logical_and(high, g < groups - 1))
     other = jnp.where(low, jnp.maximum(g - 1, 0), jnp.minimum(g + 1, groups - 1))
     plane = 3 + t
     far_plane = jnp.where(low, SPAN + 3 + t, jnp.maximum(t - (strips - 3), 0))
@@ -275,7 +295,7 @@
     def _(k):
         near(k).start()
 
-    cube[plane] = slab[pl.ds(2 * t, 3)]
+    pltpu.make_async_copy(slab.at[pl.ds(2 * t, 3)], cube.at[plane], recv_sem.at[plane]).start()
 
     for load in loads[1:]:
         load.wait()
@@ -286,30 +306,39 @@
     def arrived(p):
         pltpu.make_async_copy(cube.at[p], cube.at[p], recv_sem.at[p]).wait()
 
-    @pl.loop(1, strips)
-    def _(k):
-        arrived(3 + lax.rem(t + k, strips))
-
-    def far_channels():
-        @pl.when(g > 0)
-        def _():
-            for p in range(3):
+    def arrive(side):
+        if side == "inner":
+            @pl.loop(5, SPAN)
+            def _(p):
                 arrived(p)
-
-        @pl.when(g == 0)
-        def _():
-            cube[0:3] = jnp.zeros((3, 3, 8, 128), BF)
-
-        @pl.when(g < groups - 1)
-        def _():
-            for p in (SPAN + 3, SPAN + 4):
+        elif side == "upper":
+            for p in (SPAN, SPAN + 1, SPAN + 2):
                 arrived(p)
 
-        @pl.when(g == groups - 1)
-        def _():
-            cube[SPAN + 3 : SPAN + 5] = jnp.zeros((2, 3, 8, 128), BF)
-
-    two_layers((groups, strips, g, t), cube, far_channels, b1, b2, x1, x2, l2, x3, w1, w2)
+            @pl.when(g < groups - 1)
+            def _():
+                for p in (SPAN + 3, SPAN + 4):
+                    arrived(p)
+
+            @pl.when(g == groups - 1)
+            def _():
+                cube[SPAN + 3 : SPAN + 5] = jnp.zeros((2, 3, 8, 128), BF)
+        else:
+            for p in (3, 4):
+                arrived(p)
+
+            @pl.when(g > 0)
+            def _():
+                for p in range(3):
+                    arrived(p)
+
+            @pl.when(g == 0)
+            def _():
+                cube[0:3] = jnp.zeros((3, 3, 8, 128), BF)
+
+    all_layers(
+        (groups, strips, g, t), cube, arrive, b1, b2, bias3, x1, x2, l2, x3_upper, x3, w1, w2, w3, upper
+    )
 
     @pl.loop(1, strips)
     def _(k):
@@ -322,7 +351,8 @@
             far(k).wait_send()
 
 
-X3_SHAPE = ((SPAN // 2 + 1) * K3, 128)
+X3_SHAPE = (5 * K3, 128)
+HALF_SHAPE = (16, SPAN // 4, SPAN // 2, 64)
 WEIGHT_SCRATCH = [
     pltpu.VMEM((128, 128), F32),
     pltpu.VMEM((8, 1408), F32),
@@ -334,6 +364,7 @@
     pltpu.VMEM((PLANES * K1, 128), BF),
     pltpu.VMEM((F1 * K2, 128), BF),
     pltpu.VMEM((F2, 8 * Y2, 128), F32),
+    pltpu.VMEM(X3_SHAPE, BF),
 ]
 
 
@@ -351,9 +382,10 @@
             jax.ShapeDtypeStruct(X3_SHAPE, BF),
             jax.ShapeDtypeStruct((128, 1280), BF),
             jax.ShapeDtypeStruct((128, 128), F32),
+            jax.ShapeDtypeStruct(HALF_SHAPE, BF),
         ],
         in_specs=[pl.BlockSpec(memory_space=pltpu.HBM)] * len(operands),
-        out_specs=[vmem] * 3,
+        out_specs=[vmem] * 4,
         scratch_shapes=[
             pltpu.VMEM((height, 128), F32),
             pltpu.VMEM((height + 16, 128), F32),
@@ -378,31 +410,29 @@
     )(*operands)
 
 
-def third_kernel(x3, w3, bias3, out):
+def third_kernel(x3, w3, bias3, upper, out, lower, sem):
     quarter = SPAN // 4
-    for f in range(0, quarter, 2):
-        data = jnp.concatenate(
-            [x3[2 * h * K3 : (2 * h + 3) * K3, :] for h in (f, f + 1)], axis=1
-        )
-        sums = jnp.dot(w3[:, 0 : 3 * K3], data, preferred_element_type=F32)
-        for n, h in enumerate((f, f + 1)):
-            values = leaky(sums[:, 128 * n : 128 * (n + 1)] + bias3[...])
-            out[:, h, :, :] = values[:, 0:64].reshape(16, 8, 64).astype(BF)
-            swapped = pltpu.roll(values, 64, 1)
-            out[:, h + quarter, :, :] = swapped[:, 0:64].reshape(16, 8, 64).astype(BF)
-
-
-def third_layer(x3, w3, bias3):
+    done = pltpu.make_async_copy(upper, out.at[:, quarter : 2 * quarter], sem.at[0])
+    done.start()
+    third_matmul(x3, 0, w3, bias3, lower)
+    rest = pltpu.make_async_copy(lower, out.at[:, 0:quarter], sem.at[1])
+    rest.start()
+    done.wait()
+    rest.wait()
+
+
+def third_layer(x3, w3, bias3, upper):
     vmem = pl.BlockSpec(memory_space=pltpu.VMEM)
     half = SPAN // 2
     return pl.pallas_call(
         third_kernel,
         out_shape=jax.ShapeDtypeStruct((16, half, half, 64), BF),
-        in_specs=[vmem] * 3,
-        out_specs=vmem,
+        in_specs=[vmem] * 4,
+        out_specs=pl.BlockSpec(memory_space=pl.ANY),
+        scratch_shapes=[pltpu.VMEM(HALF_SHAPE, BF), pltpu.SemaphoreType.DMA((2,))],
         compiler_params=pltpu.CompilerParams(vmem_limit_bytes=8 << 20),
         name="third_layer",
-    )(x3, w3, bias3)
+    )(x3, w3, bias3, upper)
 
 
 def body(sky_cube, kernel_one, bias_one, kernel_two, bias_two, kernel_three, bias_three):

time: 16.1 us -> 15.8 us (0.981)
  the two profiles are of different devices: /device:TPU:15 before, /device:TPU:7 now
where the time goes in v3:
time: 15.8 us; the launch traced here: 15.7 us
  Pallas kernels  15.7 us (99%)
    pallas_call x1, Pallas kernels, first_layers(): pl.pallas_call(spread_kernel, out_shape=[jax.ShapeDtypeStruct(X3_SHAPE, B...  14.7 us
    pallas_call x1, Pallas kernels, third_layer(): pl.pallas_call(third_kernel, out_shape=jax.ShapeDtypeStruct((16, half, ha...  1.02 us

profile of v3, /device:TPU:7, one launch (start us, length us, event | category | flops | bytes accessed | tf_op | source)
XLA Modules:
  0.0 15.7 jit_solution(6051942582601933892)
XLA Ops:
  0.0 14.7 %first_layers.1 = (bf16[2080,128]{1,0:T(8,128)(2,1)S(1)}, bf16[128,1280]{1,0:T(8,128)(2,1)S(1)}, f32[128,128]{1,0:T(8,128)S(1)}, bf16[16,4,8,64]{3,2,1,0:T(8,128)(2,1)S(1)}) custom-call(f32[1,256,128]{2,1,0:T(8,128)} %sky.1, bf16[1,3,3,3,8]{4,3,2,1,0:T(4,128)(2,1)} %bitcast.5, bf16[3,3,3,8,8]{4,3,2,1,0:T(8,128)(2,1)} %bitcast.3, ...), custom_call_target="tpu_custom_call" | custom-call | tf_op jit(solution)/shard_map/first_layers/pallas_call | solution.py:379
  14.7 1.0 %third_layer.1 = bf16[16,8,8,64]{3,2,1,0:T(8,128)(2,1)} custom-call(bf16[2080,128]{1,0:T(8,128)(2,1)S(1)} %get-tuple-element.9.x3, bf16[128,1280]{1,0:T(8,128)(2,1)S(1)} %get-tuple-element.10.w3, f32[128,128]{1,0:T(8,128)S(1)} %get-tuple-element.11.bias3, bf16[16,4,8,64]{3,2,1,0:T(8,128)(2,1)S(1)} %get-tuple-element.12.upper), custom_call_target="tpu_custom_call" | custom-call | tf_op jit(solution)/shard_map/third_layer/pallas_call | solution.py:427

commit v4 on v3

--- a/solution.py
+++ b/solution.py
@@ -118,7 +118,11 @@
         out[:, n + 2, :, :] = swapped[:, 0:64].reshape(16, 8, 64).astype(BF)
 
 
-def all_layers(place, cube, arrive, b1, b2, bias3, x1, x2, l2, x3_upper, x3, w1, w2, w3, upper):
+def lower_last(g):
+    return lax.rem(g, 4) == 0
+
+
+def all_layers(place, cube, arrive, b1, b2, bias3, x1, x2, l2, x3_early, x3, w1, w2, w3, early):
     groups, strips, g, t = place
     first_g, last_g = one_if(g > 0), one_if(g < groups - 1)
     first_t, last_t = one_if(t > 0), one_if(t < strips - 1)
@@ -174,6 +178,42 @@
         )
         to[at * K3 : (at + 1) * K3, :] = block.astype(BF)
 
+    def lower_side(to):
+        arrive("lower near")
+        operand(3)
+        operand(4)
+        layer_one(3, 4)
+        layer_two(3, 4)
+        joined(to, 3, 3)
+        joined(to, 4, 4)
+        arrive("lower far")
+        for f in range(3):
+            operand(f)
+        layer_one(1, 2)
+        layer_one(0)
+        layer_two(1, 2)
+        layer_two(0)
+        for n in range(3):
+            joined(to, n, n)
+
+    def upper_side(to):
+        arrive("upper near")
+        for f in (SPAN, SPAN + 1, SPAN + 2):
+            operand(f)
+        layer_one(13, 14)
+        layer_one(15, 16)
+        layer_two(11, 12)
+        layer_two(13, 14)
+        for n in range(3):
+            joined(to, n, 8 + n)
+        arrive("upper far")
+        operand(SPAN + 3)
+        operand(SPAN + 4)
+        layer_one(17, 18)
+        layer_two(15, 16)
+        joined(to, 3, 11)
+        joined(to, 4, 12)
+
     arrive("inner")
     for f in range(5, SPAN):
         operand(f)
@@ -181,39 +221,33 @@
         layer_one(f, f + 1)
     for f in (5, 7, 9):
         layer_two(f, f + 1)
-    arrive("upper")
-    for f in range(SPAN, PLANES):
-        operand(f)
-    for f in (13, 15, 17):
-        layer_one(f, f + 1)
-    for f in (11, 13, 15):
-        layer_two(f, f + 1)
-    for n in range(5):
-        joined(x3_upper, n, 8 + n)
-    third_matmul(x3_upper, 0, w3, bias3, upper)
-    arrive("lower")
-    for f in range(5):
-        operand(f)
-    layer_one(0, 1)
-    layer_one(2, 3)
-    layer_one(4)
-    layer_two(0, 1)
-    layer_two(2, 3)
-    layer_two(4)
-    for n in range(5):
-        joined(x3, n, n)
+
+    @pl.when(lower_last(g))
+    def _():
+        upper_side(x3_early)
+        third_matmul(x3_early, 0, w3, bias3, early)
+        lower_side(x3)
+
+    @pl.when(jnp.logical_not(lower_last(g)))
+    def _():
+        lower_side(x3_early)
+        third_matmul(x3_early, 0, w3, bias3, early)
+        upper_side(x3)
 
 
 def spread_kernel(
     sky, k1_in, k2_in, k3_in, b1_in, b2_in, b3_in,
-    x3, w3, bias3, upper,
-    raw, moved, slab, cube, k1, k2, k3, b1, b2, b3, stack1, base2, stack3, w1, w2, x1, x2, l2, x3_upper,
+    x3, w3, bias3, early,
+    raw, moved, slab, cube, k1, k2, k3, b1, b2, b3, stack1, base2, stack3, w1, w2, x1, x2, l2, x3_early,
     in_sem, send_sem, recv_sem,
 ):
     groups, strips = lax.axis_size("freq"), lax.axis_size("tile")
     g, t = lax.axis_index("freq"), lax.axis_index("tile")
     height = raw.shape[0]
 
+    pairs = [(sky.at[0], raw), (k1_in, k1), (k2_in, k2), (k3_in, k3), (b1_in, b1), (b2_in, b2), (b3_in, b3)]
+    loads = [pltpu.make_async_copy(a, b, in_sem.at[n]) for n, (a, b) in enumerate(pairs)]
+    loads[0].start()
     barrier = pltpu.get_barrier_semaphore()
 
     def greet(group, strip):
@@ -233,9 +267,7 @@
     def _(k):
         greet(g, lax.rem(t + k, strips))
 
-    pairs = [(sky.at[0], raw), (k1_in, k1), (k2_in, k2), (k3_in, k3), (b1_in, b1), (b2_in, b2), (b3_in, b3)]
-    loads = [pltpu.make_async_copy(a, b, in_sem.at[n]) for n, (a, b) in enumerate(pairs)]
-    for load in loads:
+    for load in loads[1:]:
         load.start()
 
     lane = iota((128, 128), 1)
@@ -275,7 +307,8 @@
         )
 
     def far(k):
-        strip = lax.rem(t + k, strips)
+        pair = k // 2
+        strip = lax.rem(pair, 2) * (strips // 2) + pair // 2 * 2 + lax.rem(k, 2)
         return pltpu.make_async_remote_copy(
             src_ref=slab.at[pl.ds(2 * strip, 3)],
             dst_ref=cube.at[far_plane],
@@ -311,10 +344,13 @@
             @pl.loop(5, SPAN)
             def _(p):
                 arrived(p)
-        elif side == "upper":
+        elif side == "upper near":
             for p in (SPAN, SPAN + 1, SPAN + 2):
                 arrived(p)
-
+        elif side == "lower near":
+            for p in (3, 4):
+                arrived(p)
+        elif side == "upper far":
             @pl.when(g < groups - 1)
             def _():
                 for p in (SPAN + 3, SPAN + 4):
@@ -324,9 +360,6 @@
             def _():
                 cube[SPAN + 3 : SPAN + 5] = jnp.zeros((2, 3, 8, 128), BF)
         else:
-            for p in (3, 4):
-                arrived(p)
-
             @pl.when(g > 0)
             def _():
                 for p in range(3):
@@ -337,7 +370,7 @@
                 cube[0:3] = jnp.zeros((3, 3, 8, 128), BF)
 
     all_layers(
-        (groups, strips, g, t), cube, arrive, b1, b2, bias3, x1, x2, l2, x3_upper, x3, w1, w2, w3, upper
+        (groups, strips, g, t), cube, arrive, b1, b2, bias3, x1, x2, l2, x3_early, x3, w1, w2, w3, early
     )
 
     @pl.loop(1, strips)
@@ -410,18 +443,20 @@
     )(*operands)
 
 
-def third_kernel(x3, w3, bias3, upper, out, lower, sem):
+def third_kernel(x3, w3, bias3, early, out, late, sem):
     quarter = SPAN // 4
-    done = pltpu.make_async_copy(upper, out.at[:, quarter : 2 * quarter], sem.at[0])
+    lower_is_late = lower_last(lax.axis_index("freq"))
+    early_at = jnp.where(lower_is_late, quarter, 0)
+    done = pltpu.make_async_copy(early, out.at[:, pl.ds(early_at, quarter)], sem.at[0])
     done.start()
-    third_matmul(x3, 0, w3, bias3, lower)
-    rest = pltpu.make_async_copy(lower, out.at[:, 0:quarter], sem.at[1])
+    third_matmul(x3, 0, w3, bias3, late)
+    rest = pltpu.make_async_copy(late, out.at[:, pl.ds(quarter - early_at, quarter)], sem.at[1])
     rest.start()
     done.wait()
     rest.wait()
 
 
-def third_layer(x3, w3, bias3, upper):
+def third_layer(x3, w3, bias3, early):
     vmem = pl.BlockSpec(memory_space=pltpu.VMEM)
     half = SPAN // 2
     return pl.pallas_call(
@@ -432,7 +467,7 @@
         scratch_shapes=[pltpu.VMEM(HALF_SHAPE, BF), pltpu.SemaphoreType.DMA((2,))],
         compiler_params=pltpu.CompilerParams(vmem_limit_bytes=8 << 20),
         name="third_layer",
-    )(x3, w3, bias3, upper)
+    )(x3, w3, bias3, early)
 
 
 def body(sky_cube, kernel_one, bias_one, kernel_two, bias_two, kernel_three, bias_three):

time: 15.8 us -> 17 us (1.076)
  Pallas kernels: 15.7 us -> 16.9 us
    pallas_call x1, Pallas kernels: 14.7 us -> 15.8 us  [first_layers(): pl.pallas_call(spread_kernel, out_shape=[jax.ShapeDtypeStruct(X3_SHAPE, B...]
where the time goes in v4:
time: 17 us; the launch traced here: 16.9 us
  Pallas kernels  16.9 us (99%)
    pallas_call x1, Pallas kernels, first_layers(): pl.pallas_call(spread_kernel, out_shape=[jax.ShapeDtypeStruct(X3_SHAPE, B...  15.8 us
    pallas_call x1, Pallas kernels, third_layer(): pl.pallas_call(third_kernel, out_shape=jax.ShapeDtypeStruct((16, half, ha...  1.02 us

profile of v4, /device:TPU:7, one launch (start us, length us, event | category | flops | bytes accessed | tf_op | source)
XLA Modules:
  0.0 16.9 jit_solution(10261126211663707403)
XLA Ops:
  0.0 15.8 %first_layers.1 = (bf16[2080,128]{1,0:T(8,128)(2,1)S(1)}, bf16[128,1280]{1,0:T(8,128)(2,1)S(1)}, f32[128,128]{1,0:T(8,128)S(1)}, bf16[16,4,8,64]{3,2,1,0:T(8,128)(2,1)S(1)}) custom-call(f32[1,256,128]{2,1,0:T(8,128)} %sky.1, bf16[1,3,3,3,8]{4,3,2,1,0:T(4,128)(2,1)} %bitcast.5, bf16[3,3,3,8,8]{4,3,2,1,0:T(8,128)(2,1)} %bitcast.3, ...), custom_call_target="tpu_custom_call" | custom-call | tf_op jit(solution)/shard_map/first_layers/pallas_call | solution.py:412
  15.9 1.0 %third_layer.1 = bf16[16,8,8,64]{3,2,1,0:T(8,128)(2,1)} custom-call(bf16[2080,128]{1,0:T(8,128)(2,1)S(1)} %get-tuple-element.9.x3, bf16[128,1280]{1,0:T(8,128)(2,1)S(1)} %get-tuple-element.10.w3, f32[128,128]{1,0:T(8,128)S(1)} %get-tuple-element.11.bias3, bf16[16,4,8,64]{3,2,1,0:T(8,128)(2,1)S(1)} %get-tuple-element.12.early), custom_call_target="tpu_custom_call" | custom-call | tf_op jit(solution)/shard_map/third_layer/pallas_call | solution.py:462

commit v5 on v4

--- a/solution.py
+++ b/solution.py
@@ -106,9 +106,9 @@
     ).astype(BF)
 
 
-def third_matmul(x3, first, w3, bias3, out):
+def third_matmul(x3, start, w3, bias3, out):
     data = jnp.concatenate(
-        [x3[h * K3 : (h + 3) * K3, :] for h in (first, first + 2)], axis=1
+        [x3[start + h * K3 : start + (h + 3) * K3, :] for h in (0, 2)], axis=1
     )
     sums = jnp.dot(w3[:, 0 : 3 * K3], data, preferred_element_type=F32)
     for n in range(2):
@@ -122,49 +122,50 @@
     return lax.rem(g, 4) == 0
 
 
-def all_layers(place, cube, arrive, b1, b2, bias3, x1, x2, l2, x3_early, x3, w1, w2, w3, early):
+def rows_at(index, block, count):
+    return pl.ds(pl.multiple_of(index * block, 16), count)
+
+
+def all_layers(place, cube, ready, b1, b2, bias3, x1, x2, l2, x3, w1, w2, w3, early):
     groups, strips, g, t = place
     first_g, last_g = one_if(g > 0), one_if(g < groups - 1)
     first_t, last_t = one_if(t > 0), one_if(t < strips - 1)
+    low_last = lower_last(g)
 
     def operand(f):
         pieces = beside(cube[f].reshape(ROWS, 128).astype(F32))
         block = jnp.concatenate([*pieces, jnp.zeros((K1 - 3 * ROWS, 128), F32)], axis=0)
-        x1[f * K1 : (f + 1) * K1, :] = block.astype(BF)
+        x1[rows_at(f, K1, K1), :] = block.astype(BF)
 
     bias1 = column_of(b1, 8 * Y1, 8)
     row = iota((8 * Y1, 128), 0)
     keep1 = jnp.where(row < 16, first_t, jnp.where(row >= 8 * (Y1 - 1), last_t, 1.0))
-
-    def layer_one(*fs):
-        data = jnp.concatenate([x1[h * K1 : (h + 3) * K1, :] for h in fs], axis=1)
+    bias2 = column_of(b2, 8 * Y2, 8)
+    keep2 = jnp.where(iota((8 * Y2, 128), 0) < 8, first_t, 1.0)
+
+    def layer_one(f):
+        data = jnp.concatenate([x1[rows_at(h, K1, 3 * K1), :] for h in (f, f + 1)], axis=1)
         sums = jnp.dot(w1[0 : 8 * Y1, 0 : 3 * K1], data, preferred_element_type=F32)
-        for n, h in enumerate(fs):
-            values = leaky(sums[:, 128 * n : 128 * (n + 1)] + bias1) * keep1
-            if h < 2:
-                values = values * first_g
-            if h == F1 - 1:
-                values = values * last_g
+        for n in range(2):
+            h = f + n
+            inside = jnp.where(h < 2, first_g, jnp.where(h == F1 - 1, last_g, 1.0))
+            values = leaky(sums[:, 128 * n : 128 * (n + 1)] + bias1) * (keep1 * inside)
             block = jnp.concatenate(
                 [*beside(values), jnp.zeros((K2 - 24 * Y1, 128), F32)], axis=0
             )
-            x2[h * K2 : (h + 1) * K2, :] = block.astype(BF)
-
-    bias2 = column_of(b2, 8 * Y2, 8)
-    keep2 = jnp.where(iota((8 * Y2, 128), 0) < 8, first_t, 1.0)
-
-    def layer_two(*fs):
-        data = jnp.concatenate([x2[h * K2 : (h + 3) * K2, :] for h in fs], axis=1)
+            x2[rows_at(h, K2, K2), :] = block.astype(BF)
+
+    def layer_two(f):
+        data = jnp.concatenate([x2[rows_at(h, K2, 3 * K2), :] for h in (f, f + 1)], axis=1)
         sums = jnp.dot(w2[0 : 8 * Y2, 0 : 3 * K2], data, preferred_element_type=F32)
-        for n, h in enumerate(fs):
-            values = leaky(sums[:, 128 * n : 128 * (n + 1)] + bias2) * keep2
-            if h == 0:
-                values = values * first_g
-            l2[h] = values
+        for n in range(2):
+            inside = jnp.where(f + n == 0, first_g, 1.0)
+            values = leaky(sums[:, 128 * n : 128 * (n + 1)] + bias2) * (keep2 * inside)
+            l2[f + n] = values
 
     lane = iota((8 * Y2, 128), 1)
 
-    def joined(to, at, f):
+    def joined(at, f):
         lower, upper = l2[f], l2[f + 4]
         before = jnp.where(lane < 64, pltpu.roll(lower, 65, 1), pltpu.roll(upper, 1, 1))
         block = jnp.concatenate(
@@ -176,69 +177,52 @@
             ],
             axis=0,
         )
-        to[at * K3 : (at + 1) * K3, :] = block.astype(BF)
-
-    def lower_side(to):
-        arrive("lower near")
-        operand(3)
-        operand(4)
-        layer_one(3, 4)
-        layer_two(3, 4)
-        joined(to, 3, 3)
-        joined(to, 4, 4)
-        arrive("lower far")
-        for f in range(3):
-            operand(f)
-        layer_one(1, 2)
-        layer_one(0)
-        layer_two(1, 2)
-        layer_two(0)
-        for n in range(3):
-            joined(to, n, n)
-
-    def upper_side(to):
-        arrive("upper near")
-        for f in (SPAN, SPAN + 1, SPAN + 2):
-            operand(f)
-        layer_one(13, 14)
-        layer_one(15, 16)
-        layer_two(11, 12)
-        layer_two(13, 14)
-        for n in range(3):
-            joined(to, n, 8 + n)
-        arrive("upper far")
-        operand(SPAN + 3)
-        operand(SPAN + 4)
-        layer_one(17, 18)
-        layer_two(15, 16)
-        joined(to, 3, 11)
-        joined(to, 4, 12)
-
-    arrive("inner")
-    for f in range(5, SPAN):
-        operand(f)
-    for f in (5, 7, 9, 11):
-        layer_one(f, f + 1)
-    for f in (5, 7, 9):
-        layer_two(f, f + 1)
-
-    @pl.when(lower_last(g))
-    def _():
-        upper_side(x3_early)
-        third_matmul(x3_early, 0, w3, bias3, early)
-        lower_side(x3)
-
-    @pl.when(jnp.logical_not(lower_last(g)))
-    def _():
-        lower_side(x3_early)
-        third_matmul(x3_early, 0, w3, bias3, early)
-        upper_side(x3)
+        x3[rows_at(at, K3, K3), :] = block.astype(BF)
+
+    for p in (5, 6):
+        ready(p)
+        operand(p)
+
+    lower_from = jnp.where(low_last, 7, 4)
+
+    @pl.loop(0, 2)
+    def _(half):
+        @pl.loop(7 * half, 7 + 3 * half)
+        def _(step):
+            low = jnp.logical_and(step >= lower_from, step < lower_from + 3)
+            f_low = jnp.maximum(3 - 2 * (step - lower_from), 0)
+            f_up = 5 + 2 * jnp.where(step < lower_from, step, step - 3)
+            f = jnp.where(low, f_low, f_up)
+            new = jnp.where(low, f_low, f_up + 2)
+            ready(new)
+
+            @pl.when(new > 0)
+            def _():
+                ready(new + 1)
+
+            operand(new)
+            operand(new + 1)
+            layer_one(f)
+
+            @pl.when(step > 0)
+            def _():
+                layer_two(jnp.where(low, f_low, f_up - 2))
+
+        base = jnp.where(low_last, 8 - 8 * half, 8 * half)
+
+        @pl.loop(0, 5)
+        def _(n):
+            joined(5 * half + n, base + n)
+
+        @pl.when(half == 0)
+        def _():
+            third_matmul(x3, 0, w3, bias3, early)
 
 
 def spread_kernel(
     sky, k1_in, k2_in, k3_in, b1_in, b2_in, b3_in,
     x3, w3, bias3, early,
-    raw, moved, slab, cube, k1, k2, k3, b1, b2, b3, stack1, base2, stack3, w1, w2, x1, x2, l2, x3_early,
+    raw, moved, slab, cube, k1, k2, k3, b1, b2, b3, stack1, base2, stack3, w1, w2, x1, x2, l2,
     in_sem, send_sem, recv_sem,
 ):
     groups, strips = lax.axis_size("freq"), lax.axis_size("tile")
@@ -339,38 +323,22 @@
     def arrived(p):
         pltpu.make_async_copy(cube.at[p], cube.at[p], recv_sem.at[p]).wait()
 
-    def arrive(side):
-        if side == "inner":
-            @pl.loop(5, SPAN)
-            def _(p):
-                arrived(p)
-        elif side == "upper near":
-            for p in (SPAN, SPAN + 1, SPAN + 2):
-                arrived(p)
-        elif side == "lower near":
-            for p in (3, 4):
-                arrived(p)
-        elif side == "upper far":
-            @pl.when(g < groups - 1)
-            def _():
-                for p in (SPAN + 3, SPAN + 4):
-                    arrived(p)
-
-            @pl.when(g == groups - 1)
-            def _():
-                cube[SPAN + 3 : SPAN + 5] = jnp.zeros((2, 3, 8, 128), BF)
-        else:
-            @pl.when(g > 0)
-            def _():
-                for p in range(3):
-                    arrived(p)
-
-            @pl.when(g == 0)
-            def _():
-                cube[0:3] = jnp.zeros((3, 3, 8, 128), BF)
+    def ready(p):
+        missing = jnp.logical_or(
+            jnp.logical_and(p < 3, g == 0),
+            jnp.logical_and(p >= SPAN + 3, g == groups - 1),
+        )
+
+        @pl.when(missing)
+        def _():
+            cube[p] = jnp.zeros((3, 8, 128), BF)
+
+        @pl.when(jnp.logical_not(missing))
+        def _():
+            arrived(p)
 
     all_layers(
-        (groups, strips, g, t), cube, arrive, b1, b2, bias3, x1, x2, l2, x3_early, x3, w1, w2, w3, early
+        (groups, strips, g, t), cube, ready, b1, b2, bias3, x1, x2, l2, x3, w1, w2, w3, early
     )
 
     @pl.loop(1, strips)
@@ -384,7 +352,7 @@
             far(k).wait_send()
 
 
-X3_SHAPE = (5 * K3, 128)
+X3_SHAPE = (10 * K3, 128)
 HALF_SHAPE = (16, SPAN // 4, SPAN // 2, 64)
 WEIGHT_SCRATCH = [
     pltpu.VMEM((128, 128), F32),
@@ -397,7 +365,6 @@
     pltpu.VMEM((PLANES * K1, 128), BF),
     pltpu.VMEM((F1 * K2, 128), BF),
     pltpu.VMEM((F2, 8 * Y2, 128), F32),
-    pltpu.VMEM(X3_SHAPE, BF),
 ]
 
 
@@ -449,7 +416,7 @@
     early_at = jnp.where(lower_is_late, quarter, 0)
     done = pltpu.make_async_copy(early, out.at[:, pl.ds(early_at, quarter)], sem.at[0])
     done.start()
-    third_matmul(x3, 0, w3, bias3, late)
+    third_matmul(x3, 5 * K3, w3, bias3, late)
     rest = pltpu.make_async_copy(late, out.at[:, pl.ds(quarter - early_at, quarter)], sem.at[1])
     rest.start()
     done.wait()

time: 17 us -> 20.7 us (1.22)
  Pallas kernels: 16.9 us -> 20.6 us
    pallas_call x1, Pallas kernels: 15.8 us -> 19.6 us  [first_layers(): pl.pallas_call(spread_kernel, out_shape=[jax.ShapeDtypeStruct(X3_SHAPE, B...]
where the time goes in v5:
time: 20.7 us; the launch traced here: 20.6 us
  Pallas kernels  20.6 us (100%)
    pallas_call x1, Pallas kernels, first_layers(): pl.pallas_call(spread_kernel, out_shape=[jax.ShapeDtypeStruct(X3_SHAPE, B...  19.6 us
    pallas_call x1, Pallas kernels, third_layer(): pl.pallas_call(third_kernel, out_shape=jax.ShapeDtypeStruct((16, half, ha...  1.02 us

profile of v5, /device:TPU:7, one launch (start us, length us, event | category | flops | bytes accessed | tf_op | source)
XLA Modules:
  0.0 20.6 jit_solution(3740084679332034347)
XLA Ops:
  0.0 19.6 %first_layers.1 = (bf16[4160,128]{1,0:T(8,128)(2,1)S(1)}, bf16[128,1280]{1,0:T(8,128)(2,1)S(1)}, f32[128,128]{1,0:T(8,128)S(1)}, bf16[16,4,8,64]{3,2,1,0:T(8,128)(2,1)S(1)}) custom-call(f32[1,256,128]{2,1,0:T(8,128)} %sky.1, bf16[1,3,3,3,8]{4,3,2,1,0:T(4,128)(2,1)} %bitcast.5, bf16[3,3,3,8,8]{4,3,2,1,0:T(8,128)(2,1)} %bitcast.3, ...), custom_call_target="tpu_custom_call" | custom-call | tf_op jit(solution)/shard_map/first_layers/pallas_call | solution.py:379
  19.6 1.0 %third_layer.1 = bf16[16,8,8,64]{3,2,1,0:T(8,128)(2,1)} custom-call(bf16[4160,128]{1,0:T(8,128)(2,1)S(1)} %get-tuple-element.9.x3, bf16[128,1280]{1,0:T(8,128)(2,1)S(1)} %get-tuple-element.10.w3, f32[128,128]{1,0:T(8,128)S(1)} %get-tuple-element.11.bias3, bf16[16,4,8,64]{3,2,1,0:T(8,128)(2,1)S(1)} %get-tuple-element.12.early), custom_call_target="tpu_custom_call" | custom-call | tf_op jit(solution)/shard_map/third_layer/pallas_call | solution.py:429

commit v6 on v3

--- a/solution.py
+++ b/solution.py
@@ -118,7 +118,7 @@
         out[:, n + 2, :, :] = swapped[:, 0:64].reshape(16, 8, 64).astype(BF)
 
 
-def all_layers(place, cube, arrive, b1, b2, bias3, x1, x2, l2, x3_upper, x3, w1, w2, w3, upper):
+def layer_steps(place, cube, arrive, b1, b2, bias3, x1, x2, l2, x3_upper, x3, w1, w2, w3, upper):
     groups, strips, g, t = place
     first_g, last_g = one_if(g > 0), one_if(g < groups - 1)
     first_t, last_t = one_if(t > 0), one_if(t < strips - 1)
@@ -174,34 +174,51 @@
         )
         to[at * K3 : (at + 1) * K3, :] = block.astype(BF)
 
-    arrive("inner")
-    for f in range(5, SPAN):
-        operand(f)
-    for f in (5, 7, 9, 11):
-        layer_one(f, f + 1)
-    for f in (5, 7, 9):
-        layer_two(f, f + 1)
-    arrive("upper")
-    for f in range(SPAN, PLANES):
-        operand(f)
-    for f in (13, 15, 17):
-        layer_one(f, f + 1)
-    for f in (11, 13, 15):
-        layer_two(f, f + 1)
-    for n in range(5):
-        joined(x3_upper, n, 8 + n)
-    third_matmul(x3_upper, 0, w3, bias3, upper)
-    arrive("lower")
-    for f in range(5):
-        operand(f)
-    layer_one(0, 1)
-    layer_one(2, 3)
-    layer_one(4)
-    layer_two(0, 1)
-    layer_two(2, 3)
-    layer_two(4)
-    for n in range(5):
-        joined(x3, n, n)
+    def inner():
+        arrive("inner")
+        for f in range(5, SPAN):
+            operand(f)
+        for f in (5, 7, 9, 11):
+            layer_one(f, f + 1)
+        for f in (5, 7, 9):
+            layer_two(f, f + 1)
+
+    def rest():
+        arrive("upper near")
+        for f in (SPAN, SPAN + 1, SPAN + 2):
+            operand(f)
+        layer_one(13, 14)
+        layer_one(15, 16)
+        layer_two(11, 12)
+        layer_two(13, 14)
+        for n in range(3):
+            joined(x3_upper, n, 8 + n)
+        arrive("lower near")
+        operand(3)
+        operand(4)
+        layer_one(3, 4)
+        layer_two(3, 4)
+        joined(x3, 3, 3)
+        joined(x3, 4, 4)
+        arrive("upper far")
+        operand(SPAN + 3)
+        operand(SPAN + 4)
+        layer_one(17, 18)
+        layer_two(15, 16)
+        joined(x3_upper, 3, 11)
+        joined(x3_upper, 4, 12)
+        third_matmul(x3_upper, 0, w3, bias3, upper)
+        arrive("lower far")
+        for f in range(3):
+            operand(f)
+        layer_one(1, 2)
+        layer_one(0)
+        layer_two(1, 2)
+        layer_two(0)
+        for n in range(3):
+            joined(x3, n, n)
+
+    return inner, rest
 
 
 def spread_kernel(
@@ -214,6 +231,11 @@
     g, t = lax.axis_index("freq"), lax.axis_index("tile")
     height = raw.shape[0]
 
+    pairs = [(sky.at[0], raw), (k1_in, k1), (k2_in, k2), (k3_in, k3), (b1_in, b1), (b2_in, b2), (b3_in, b3)]
+    loads = [pltpu.make_async_copy(a, b, in_sem.at[n]) for n, (a, b) in enumerate(pairs)]
+    for load in loads:
+        load.start()
+
     barrier = pltpu.get_barrier_semaphore()
 
     def greet(group, strip):
@@ -232,11 +254,6 @@
     @pl.loop(1, strips)
     def _(k):
         greet(g, lax.rem(t + k, strips))
-
-    pairs = [(sky.at[0], raw), (k1_in, k1), (k2_in, k2), (k3_in, k3), (b1_in, b1), (b2_in, b2), (b3_in, b3)]
-    loads = [pltpu.make_async_copy(a, b, in_sem.at[n]) for n, (a, b) in enumerate(pairs)]
-    for load in loads:
-        load.start()
 
     lane = iota((128, 128), 1)
     column = jnp.where(lane < 64, 2 * lane, 2 * lane - 127)
@@ -254,14 +271,6 @@
     other = jnp.where(low, jnp.maximum(g - 1, 0), jnp.minimum(g + 1, groups - 1))
     plane = 3 + t
     far_plane = jnp.where(low, SPAN + 3 + t, jnp.maximum(t - (strips - 3), 0))
-
-    @pl.when(beyond)
-    def _():
-        pl.semaphore_wait(barrier, 2 * strips - 1)
-
-    @pl.when(jnp.logical_not(beyond))
-    def _():
-        pl.semaphore_wait(barrier, strips - 1)
 
     def near(k):
         strip = lax.rem(t + k, strips)
@@ -285,23 +294,25 @@
             device_id_type=MESH,
         )
 
-    @pl.when(beyond)
-    def _():
-        @pl.loop(0, strips)
+    own = pltpu.make_async_copy(slab.at[pl.ds(2 * t, 3)], cube.at[plane], recv_sem.at[plane])
+    own.start()
+
+    def send():
+        @pl.when(beyond)
+        def _():
+            pl.semaphore_wait(barrier, 2 * strips - 1)
+
+            @pl.loop(0, strips)
+            def _(k):
+                far(k).start()
+
+        @pl.when(jnp.logical_not(beyond))
+        def _():
+            pl.semaphore_wait(barrier, strips - 1)
+
+        @pl.loop(1, strips)
         def _(k):
-            far(k).start()
-
-    @pl.loop(1, strips)
-    def _(k):
-        near(k).start()
-
-    pltpu.make_async_copy(slab.at[pl.ds(2 * t, 3)], cube.at[plane], recv_sem.at[plane]).start()
-
-    for load in loads[1:]:
-        load.wait()
-    banded_weights(k1, k2, k3, stack1, base2, stack3, w1, w2, w3)
-    for o in range(16):
-        bias3[8 * o : 8 * o + 8, :] = jnp.full((8, 128), b3[o], F32)
+            near(k).start()
 
     def arrived(p):
         pltpu.make_async_copy(cube.at[p], cube.at[p], recv_sem.at[p]).wait()
@@ -311,10 +322,13 @@
             @pl.loop(5, SPAN)
             def _(p):
                 arrived(p)
-        elif side == "upper":
+        elif side == "upper near":
             for p in (SPAN, SPAN + 1, SPAN + 2):
                 arrived(p)
-
+        elif side == "lower near":
+            for p in (3, 4):
+                arrived(p)
+        elif side == "upper far":
             @pl.when(g < groups - 1)
             def _():
                 for p in (SPAN + 3, SPAN + 4):
@@ -324,9 +338,6 @@
             def _():
                 cube[SPAN + 3 : SPAN + 5] = jnp.zeros((2, 3, 8, 128), BF)
         else:
-            for p in (3, 4):
-                arrived(p)
-
             @pl.when(g > 0)
             def _():
                 for p in range(3):
@@ -336,9 +347,29 @@
             def _():
                 cube[0:3] = jnp.zeros((3, 3, 8, 128), BF)
 
-    all_layers(
+    for load in loads[1:]:
+        load.wait()
+    inner, rest = layer_steps(
         (groups, strips, g, t), cube, arrive, b1, b2, bias3, x1, x2, l2, x3_upper, x3, w1, w2, w3, upper
     )
+
+    compute_first = jnp.logical_and(jnp.logical_and(low, g > 0), lax.rem(g, 4) == 0)
+    compute_at = jnp.where(compute_first, 0, 1)
+
+    @pl.loop(0, 2)
+    def _(turn):
+        @pl.when(turn == compute_at)
+        def _():
+            banded_weights(k1, k2, k3, stack1, base2, stack3, w1, w2, w3)
+            for o in range(16):
+                bias3[8 * o : 8 * o + 8, :] = jnp.full((8, 128), b3[o], F32)
+            inner()
+
+        @pl.when(turn == 0)
+        def _():
+            send()
+
+    rest()
 
     @pl.loop(1, strips)
     def _(k):

time: 15.8 us -> 16.4 us (1.038)
  the two profiles are of different devices: /device:TPU:7 before, /device:TPU:1 now
where the time goes in v6:
time: 16.4 us; the launch traced here: 16.3 us
  Pallas kernels  16.3 us (99%)
    pallas_call x1, Pallas kernels, first_layers(): pl.pallas_call(spread_kernel, out_shape=[jax.ShapeDtypeStruct(X3_SHAPE, B...  15.3 us
    pallas_call x1, Pallas kernels, third_layer(): pl.pallas_call(third_kernel, out_shape=jax.ShapeDtypeStruct((16, half, ha...  1.02 us

profile of v6, /device:TPU:1, one launch (start us, length us, event | category | flops | bytes accessed | tf_op | source)
XLA Modules:
  0.0 16.3 jit_solution(13614973438838269296)
XLA Ops:
  0.0 15.3 %first_layers.1 = (bf16[2080,128]{1,0:T(8,128)(2,1)S(1)}, bf16[128,1280]{1,0:T(8,128)(2,1)S(1)}, f32[128,128]{1,0:T(8,128)S(1)}, bf16[16,4,8,64]{3,2,1,0:T(8,128)(2,1)S(1)}) custom-call(f32[1,256,128]{2,1,0:T(8,128)} %sky.1, bf16[1,3,3,3,8]{4,3,2,1,0:T(4,128)(2,1)} %bitcast.5, bf16[3,3,3,8,8]{4,3,2,1,0:T(8,128)(2,1)} %bitcast.3, ...), custom_call_target="tpu_custom_call" | custom-call | tf_op jit(solution)/shard_map/first_layers/pallas_call | solution.py:410
  15.3 1.0 %third_layer.1 = bf16[16,8,8,64]{3,2,1,0:T(8,128)(2,1)} custom-call(bf16[2080,128]{1,0:T(8,128)(2,1)S(1)} %get-tuple-element.9.x3, bf16[128,1280]{1,0:T(8,128)(2,1)S(1)} %get-tuple-element.10.w3, f32[128,128]{1,0:T(8,128)S(1)} %get-tuple-element.11.bias3, bf16[16,4,8,64]{3,2,1,0:T(8,128)(2,1)S(1)} %get-tuple-element.12.upper), custom_call_target="tpu_custom_call" | custom-call | tf_op jit(solution)/shard_map/third_layer/pallas_call | solution.py:458

commit v7 on v6

--- a/solution.py
+++ b/solution.py
@@ -231,29 +231,29 @@
     g, t = lax.axis_index("freq"), lax.axis_index("tile")
     height = raw.shape[0]
 
+    barrier = pltpu.get_barrier_semaphore()
+
+    def greet(group, strip):
+        pl.semaphore_signal(barrier, inc=1, device_id=(group, strip), device_id_type=MESH)
+
+    @pl.when(g < groups - 1)
+    def _():
+        for strip in (0, 1):
+            greet(g + 1, strip)
+
+    @pl.when(g > 0)
+    def _():
+        for strip in (strips - 3, strips - 2, strips - 1):
+            greet(g - 1, strip)
+
+    @pl.loop(1, strips)
+    def _(k):
+        greet(g, lax.rem(t + k, strips))
+
     pairs = [(sky.at[0], raw), (k1_in, k1), (k2_in, k2), (k3_in, k3), (b1_in, b1), (b2_in, b2), (b3_in, b3)]
     loads = [pltpu.make_async_copy(a, b, in_sem.at[n]) for n, (a, b) in enumerate(pairs)]
     for load in loads:
         load.start()
-
-    barrier = pltpu.get_barrier_semaphore()
-
-    def greet(group, strip):
-        pl.semaphore_signal(barrier, inc=1, device_id=(group, strip), device_id_type=MESH)
-
-    @pl.when(g < groups - 1)
-    def _():
-        for strip in (0, 1):
-            greet(g + 1, strip)
-
-    @pl.when(g > 0)
-    def _():
-        for strip in (strips - 3, strips - 2, strips - 1):
-            greet(g - 1, strip)
-
-    @pl.loop(1, strips)
-    def _(k):
-        greet(g, lax.rem(t + k, strips))
 
     lane = iota((128, 128), 1)
     column = jnp.where(lane < 64, 2 * lane, 2 * lane - 127)

time: 16.4 us -> 16.4 us (level)
  no operation moved by 1% of the time
where the time goes in v7:
time: 16.4 us; the launch traced here: 16.3 us
  Pallas kernels  16.3 us (99%)
    pallas_call x1, Pallas kernels, first_layers(): pl.pallas_call(spread_kernel, out_shape=[jax.ShapeDtypeStruct(X3_SHAPE, B...  15.3 us
    pallas_call x1, Pallas kernels, third_layer(): pl.pallas_call(third_kernel, out_shape=jax.ShapeDtypeStruct((16, half, ha...  1.03 us

profile of v7, /device:TPU:1, one launch (start us, length us, event | category | flops | bytes accessed | tf_op | source)
XLA Modules:
  0.0 16.3 jit_solution(7216612982088622721)
XLA Ops:
  0.0 15.3 %first_layers.1 = (bf16[2080,128]{1,0:T(8,128)(2,1)S(1)}, bf16[128,1280]{1,0:T(8,128)(2,1)S(1)}, f32[128,128]{1,0:T(8,128)S(1)}, bf16[16,4,8,64]{3,2,1,0:T(8,128)(2,1)S(1)}) custom-call(f32[1,256,128]{2,1,0:T(8,128)} %sky.1, bf16[1,3,3,3,8]{4,3,2,1,0:T(4,128)(2,1)} %bitcast.5, bf16[3,3,3,8,8]{4,3,2,1,0:T(8,128)(2,1)} %bitcast.3, ...), custom_call_target="tpu_custom_call" | custom-call | tf_op jit(solution)/shard_map/first_layers/pallas_call | solution.py:410
  15.3 1.0 %third_layer.1 = bf16[16,8,8,64]{3,2,1,0:T(8,128)(2,1)} custom-call(bf16[2080,128]{1,0:T(8,128)(2,1)S(1)} %get-tuple-element.9.x3, bf16[128,1280]{1,0:T(8,128)(2,1)S(1)} %get-tuple-element.10.w3, f32[128,128]{1,0:T(8,128)S(1)} %get-tuple-element.11.bias3, bf16[16,4,8,64]{3,2,1,0:T(8,128)(2,1)S(1)} %get-tuple-element.12.upper), custom_call_target="tpu_custom_call" | custom-call | tf_op jit(solution)/shard_map/third_layer/pallas_call | solution.py:458

commit v8 on v3

--- a/solution.py
+++ b/solution.py
@@ -55,7 +55,7 @@
     return jnp.where(inside, 1.0, 0.0).astype(F32)
 
 
-def banded_weights(k1, k2, k3, stack1, base2, stack3, w1, w2, w3):
+def first_weights(k1, k2, stack1, base2, w1, w2):
     stack1[...] = jnp.zeros(stack1.shape, F32)
     for a in range(3):
         for b in range(3):
@@ -83,6 +83,8 @@
         both = [pltpu.roll(base, 8 * s, 1) if s else base for s in (y, min(y + 1, Y2 - 1))]
         w2[8 * y : 8 * y + 16, :] = jnp.concatenate(both, axis=0).astype(BF)
 
+
+def third_weights(k3, stack3, w3):
     stack3[...] = jnp.zeros(stack3.shape, F32)
     for n, (a, b, c) in enumerate(taps()):
         stack3[8 * n : 8 * n + 8, 0:16] = k3[a, b, c].astype(F32)
@@ -191,16 +193,21 @@
     for n in range(5):
         joined(x3_upper, n, 8 + n)
     third_matmul(x3_upper, 0, w3, bias3, upper)
-    arrive("lower")
-    for f in range(5):
+    arrive("lower near")
+    operand(3)
+    operand(4)
+    layer_one(3, 4)
+    layer_two(3, 4)
+    joined(x3, 3, 3)
+    joined(x3, 4, 4)
+    arrive("lower far")
+    for f in range(3):
         operand(f)
-    layer_one(0, 1)
-    layer_one(2, 3)
-    layer_one(4)
-    layer_two(0, 1)
-    layer_two(2, 3)
-    layer_two(4)
-    for n in range(5):
+    layer_one(1, 2)
+    layer_one(0)
+    layer_two(1, 2)
+    layer_two(0)
+    for n in range(3):
         joined(x3, n, n)
 
 
@@ -233,7 +240,7 @@
     def _(k):
         greet(g, lax.rem(t + k, strips))
 
-    pairs = [(sky.at[0], raw), (k1_in, k1), (k2_in, k2), (k3_in, k3), (b1_in, b1), (b2_in, b2), (b3_in, b3)]
+    pairs = [(k1_in, k1), (k2_in, k2), (sky.at[0], raw), (k3_in, k3), (b1_in, b1), (b2_in, b2), (b3_in, b3)]
     loads = [pltpu.make_async_copy(a, b, in_sem.at[n]) for n, (a, b) in enumerate(pairs)]
     for load in loads:
         load.start()
@@ -244,6 +251,9 @@
     moved[0:8, :] = jnp.zeros((8, 128), F32)
     moved[height : height + 16, :] = jnp.zeros((16, 128), F32)
     loads[0].wait()
+    loads[1].wait()
+    first_weights(k1, k2, stack1, base2, w1, w2)
+    loads[2].wait()
     values = jnp.dot(raw[...].astype(BF), order, preferred_element_type=F32)
     moved[4 : height + 4, :] = values
     slab[...] = moved[...].reshape(slab.shape).astype(BF)
@@ -297,9 +307,9 @@
 
     pltpu.make_async_copy(slab.at[pl.ds(2 * t, 3)], cube.at[plane], recv_sem.at[plane]).start()
 
-    for load in loads[1:]:
+    for load in loads[3:]:
         load.wait()
-    banded_weights(k1, k2, k3, stack1, base2, stack3, w1, w2, w3)
+    third_weights(k3, stack3, w3)
     for o in range(16):
         bias3[8 * o : 8 * o + 8, :] = jnp.full((8, 128), b3[o], F32)
 
@@ -323,10 +333,10 @@
             @pl.when(g == groups - 1)
             def _():
                 cube[SPAN + 3 : SPAN + 5] = jnp.zeros((2, 3, 8, 128), BF)
-        else:
+        elif side == "lower near":
             for p in (3, 4):
                 arrived(p)
-
+        else:
             @pl.when(g > 0)
             def _():
                 for p in range(3):

time: 15.8 us -> 16.4 us (1.038)
  Pallas kernels: 15.7 us -> 16.3 us
    pallas_call x1, Pallas kernels: 14.7 us -> 15.2 us  [first_layers(): pl.pallas_call(spread_kernel, out_shape=[jax.ShapeDtypeStruct(X3_SHAPE, B...]
where the time goes in v8:
time: 16.4 us; the launch traced here: 16.3 us
  Pallas kernels  16.3 us (99%)
    pallas_call x1, Pallas kernels, first_layers(): pl.pallas_call(spread_kernel, out_shape=[jax.ShapeDtypeStruct(X3_SHAPE, B...  15.2 us
    pallas_call x1, Pallas kernels, third_layer(): pl.pallas_call(third_kernel, out_shape=jax.ShapeDtypeStruct((16, half, ha...  1.03 us

profile of v8, /device:TPU:7, one launch (start us, length us, event | category | flops | bytes accessed | tf_op | source)
XLA Modules:
  0.0 16.3 jit_solution(7531832963849209048)
XLA Ops:
  0.0 15.2 %first_layers.1 = (bf16[2080,128]{1,0:T(8,128)(2,1)S(1)}, bf16[128,1280]{1,0:T(8,128)(2,1)S(1)}, f32[128,128]{1,0:T(8,128)S(1)}, bf16[16,4,8,64]{3,2,1,0:T(8,128)(2,1)S(1)}) custom-call(f32[1,256,128]{2,1,0:T(8,128)} %sky.1, bf16[1,3,3,3,8]{4,3,2,1,0:T(4,128)(2,1)} %bitcast.5, bf16[3,3,3,8,8]{4,3,2,1,0:T(8,128)(2,1)} %bitcast.3, ...), custom_call_target="tpu_custom_call" | custom-call | tf_op jit(solution)/shard_map/first_layers/pallas_call | solution.py:389
  15.2 1.0 %third_layer.1 = bf16[16,8,8,64]{3,2,1,0:T(8,128)(2,1)} custom-call(bf16[2080,128]{1,0:T(8,128)(2,1)S(1)} %get-tuple-element.9.x3, bf16[128,1280]{1,0:T(8,128)(2,1)S(1)} %get-tuple-element.10.w3, f32[128,128]{1,0:T(8,128)S(1)} %get-tuple-element.11.bias3, bf16[16,4,8,64]{3,2,1,0:T(8,128)(2,1)S(1)} %get-tuple-element.12.upper), custom_call_target="tpu_custom_call" | custom-call | tf_op jit(solution)/shard_map/third_layer/pallas_call | solution.py:437

commit v9 on v8

--- a/solution.py
+++ b/solution.py
@@ -55,7 +55,7 @@
     return jnp.where(inside, 1.0, 0.0).astype(F32)
 
 
-def first_weights(k1, k2, stack1, base2, w1, w2):
+def banded_weights(k1, k2, k3, stack1, base2, stack3, w1, w2, w3):
     stack1[...] = jnp.zeros(stack1.shape, F32)
     for a in range(3):
         for b in range(3):
@@ -83,8 +83,6 @@
         both = [pltpu.roll(base, 8 * s, 1) if s else base for s in (y, min(y + 1, Y2 - 1))]
         w2[8 * y : 8 * y + 16, :] = jnp.concatenate(both, axis=0).astype(BF)
 
-
-def third_weights(k3, stack3, w3):
     stack3[...] = jnp.zeros(stack3.shape, F32)
     for n, (a, b, c) in enumerate(taps()):
         stack3[8 * n : 8 * n + 8, 0:16] = k3[a, b, c].astype(F32)
@@ -221,6 +219,13 @@
     g, t = lax.axis_index("freq"), lax.axis_index("tile")
     height = raw.shape[0]
 
+    quarter = height // 4
+    pairs = [(sky.at[0, pl.ds(n * quarter, quarter)], raw.at[pl.ds(n * quarter, quarter)]) for n in range(4)]
+    pairs += [(k1_in, k1), (k2_in, k2), (k3_in, k3), (b1_in, b1), (b2_in, b2), (b3_in, b3)]
+    loads = [pltpu.make_async_copy(a, b, in_sem.at[n]) for n, (a, b) in enumerate(pairs)]
+    for load in loads[:4]:
+        load.start()
+
     barrier = pltpu.get_barrier_semaphore()
 
     def greet(group, strip):
@@ -239,21 +244,16 @@
     @pl.loop(1, strips)
     def _(k):
         greet(g, lax.rem(t + k, strips))
-
-    pairs = [(k1_in, k1), (k2_in, k2), (sky.at[0], raw), (k3_in, k3), (b1_in, b1), (b2_in, b2), (b3_in, b3)]
-    loads = [pltpu.make_async_copy(a, b, in_sem.at[n]) for n, (a, b) in enumerate(pairs)]
-    for load in loads:
-        load.start()
 
     lane = iota((128, 128), 1)
     column = jnp.where(lane < 64, 2 * lane, 2 * lane - 127)
     order = (iota((128, 128), 0) == column).astype(F32).astype(BF)
     moved[0:8, :] = jnp.zeros((8, 128), F32)
     moved[height : height + 16, :] = jnp.zeros((16, 128), F32)
-    loads[0].wait()
-    loads[1].wait()
-    first_weights(k1, k2, stack1, base2, w1, w2)
-    loads[2].wait()
+    for load in loads[:4]:
+        load.wait()
+    for load in loads[4:]:
+        load.start()
     values = jnp.dot(raw[...].astype(BF), order, preferred_element_type=F32)
     moved[4 : height + 4, :] = values
     slab[...] = moved[...].reshape(slab.shape).astype(BF)
@@ -307,9 +307,9 @@
 
     pltpu.make_async_copy(slab.at[pl.ds(2 * t, 3)], cube.at[plane], recv_sem.at[plane]).start()
 
-    for load in loads[3:]:
+    for load in loads[4:]:
         load.wait()
-    third_weights(k3, stack3, w3)
+    banded_weights(k1, k2, k3, stack1, base2, stack3, w1, w2, w3)
     for o in range(16):
         bias3[8 * o : 8 * o + 8, :] = jnp.full((8, 128), b3[o], F32)
 
@@ -409,7 +409,7 @@
             pltpu.SMEM(b3.shape, F32),
             *WEIGHT_SCRATCH,
             *LAYER_SCRATCH,
-            pltpu.SemaphoreType.DMA((len(operands),)),
+            pltpu.SemaphoreType.DMA((len(operands) + 3,)),
             pltpu.SemaphoreType.DMA((2 * strips,)),
             pltpu.SemaphoreType.DMA((PLANES,)),
         ],

time: 16.4 us -> 16.6 us (1.012)
  no operation moved by 1% of the time
where the time goes in v9:
time: 16.6 us; the launch traced here: 16.4 us
  Pallas kernels  16.4 us (99%)
    pallas_call x1, Pallas kernels, first_layers(): pl.pallas_call(spread_kernel, out_shape=[jax.ShapeDtypeStruct(X3_SHAPE, B...  15.3 us
    pallas_call x1, Pallas kernels, third_layer(): pl.pallas_call(third_kernel, out_shape=jax.ShapeDtypeStruct((16, half, ha...  1.03 us

profile of v9, /device:TPU:7, one launch (start us, length us, event | category | flops | bytes accessed | tf_op | source)
XLA Modules:
  0.0 16.4 jit_solution(15839087947694017396)
XLA Ops:
  0.0 15.3 %first_layers.1 = (bf16[2080,128]{1,0:T(8,128)(2,1)S(1)}, bf16[128,1280]{1,0:T(8,128)(2,1)S(1)}, f32[128,128]{1,0:T(8,128)S(1)}, bf16[16,4,8,64]{3,2,1,0:T(8,128)(2,1)S(1)}) custom-call(f32[1,256,128]{2,1,0:T(8,128)} %sky.1, bf16[1,3,3,3,8]{4,3,2,1,0:T(4,128)(2,1)} %bitcast.5, bf16[3,3,3,8,8]{4,3,2,1,0:T(8,128)(2,1)} %bitcast.3, ...), custom_call_target="tpu_custom_call" | custom-call | tf_op jit(solution)/shard_map/first_layers/pallas_call | solution.py:389
  15.3 1.0 %third_layer.1 = bf16[16,8,8,64]{3,2,1,0:T(8,128)(2,1)} custom-call(bf16[2080,128]{1,0:T(8,128)(2,1)S(1)} %get-tuple-element.9.x3, bf16[128,1280]{1,0:T(8,128)(2,1)S(1)} %get-tuple-element.10.w3, f32[128,128]{1,0:T(8,128)S(1)} %get-tuple-element.11.bias3, bf16[16,4,8,64]{3,2,1,0:T(8,128)(2,1)S(1)} %get-tuple-element.12.upper), custom_call_target="tpu_custom_call" | custom-call | tf_op jit(solution)/shard_map/third_layer/pallas_call | solution.py:437

commit v10 on v3

--- a/solution.py
+++ b/solution.py
@@ -214,6 +214,13 @@
     g, t = lax.axis_index("freq"), lax.axis_index("tile")
     height = raw.shape[0]
 
+    quarter = height // 4
+    pairs = [(sky.at[0, pl.ds(n * quarter, quarter)], raw.at[pl.ds(n * quarter, quarter)]) for n in range(4)]
+    pairs += [(k1_in, k1), (k2_in, k2), (k3_in, k3), (b1_in, b1), (b2_in, b2), (b3_in, b3)]
+    loads = [pltpu.make_async_copy(a, b, in_sem.at[n]) for n, (a, b) in enumerate(pairs)]
+    for load in loads[:4]:
+        load.start()
+
     barrier = pltpu.get_barrier_semaphore()
 
     def greet(group, strip):
@@ -232,18 +239,16 @@
     @pl.loop(1, strips)
     def _(k):
         greet(g, lax.rem(t + k, strips))
-
-    pairs = [(sky.at[0], raw), (k1_in, k1), (k2_in, k2), (k3_in, k3), (b1_in, b1), (b2_in, b2), (b3_in, b3)]
-    loads = [pltpu.make_async_copy(a, b, in_sem.at[n]) for n, (a, b) in enumerate(pairs)]
-    for load in loads:
-        load.start()
 
     lane = iota((128, 128), 1)
     column = jnp.where(lane < 64, 2 * lane, 2 * lane - 127)
     order = (iota((128, 128), 0) == column).astype(F32).astype(BF)
     moved[0:8, :] = jnp.zeros((8, 128), F32)
     moved[height : height + 16, :] = jnp.zeros((16, 128), F32)
-    loads[0].wait()
+    for load in loads[:4]:
+        load.wait()
+    for load in loads[4:]:
+        load.start()
     values = jnp.dot(raw[...].astype(BF), order, preferred_element_type=F32)
     moved[4 : height + 4, :] = values
     slab[...] = moved[...].reshape(slab.shape).astype(BF)
@@ -297,7 +302,7 @@
 
     pltpu.make_async_copy(slab.at[pl.ds(2 * t, 3)], cube.at[plane], recv_sem.at[plane]).start()
 
-    for load in loads[1:]:
+    for load in loads[4:]:
         load.wait()
     banded_weights(k1, k2, k3, stack1, base2, stack3, w1, w2, w3)
     for o in range(16):
@@ -399,7 +404,7 @@
             pltpu.SMEM(b3.shape, F32),
             *WEIGHT_SCRATCH,
             *LAYER_SCRATCH,
-            pltpu.SemaphoreType.DMA((len(operands),)),
+            pltpu.SemaphoreType.DMA((len(operands) + 3,)),
             pltpu.SemaphoreType.DMA((2 * strips,)),
             pltpu.SemaphoreType.DMA((PLANES,)),
         ],

time: 15.8 us -> 16 us (1.013); the launches traced: 15.7 us -> 15.7 us
  no operation moved by 1% of the time
where the time goes in v10:
time: 16 us; the launch traced here: 15.7 us
  Pallas kernels  15.7 us (98%)
    pallas_call x1, Pallas kernels, first_layers(): pl.pallas_call(spread_kernel, out_shape=[jax.ShapeDtypeStruct(X3_SHAPE, B...  14.7 us
    pallas_call x1, Pallas kernels, third_layer(): pl.pallas_call(third_kernel, out_shape=jax.ShapeDtypeStruct((16, half, ha...  1.03 us

profile of v10, /device:TPU:7, one launch (start us, length us, event | category | flops | bytes accessed | tf_op | source)
XLA Modules:
  0.0 15.7 jit_solution(3490401021675897998)
XLA Ops:
  0.0 14.7 %first_layers.1 = (bf16[2080,128]{1,0:T(8,128)(2,1)S(1)}, bf16[128,1280]{1,0:T(8,128)(2,1)S(1)}, f32[128,128]{1,0:T(8,128)S(1)}, bf16[16,4,8,64]{3,2,1,0:T(8,128)(2,1)S(1)}) custom-call(f32[1,256,128]{2,1,0:T(8,128)} %sky.1, bf16[1,3,3,3,8]{4,3,2,1,0:T(4,128)(2,1)} %bitcast.5, bf16[3,3,3,8,8]{4,3,2,1,0:T(8,128)(2,1)} %bitcast.3, ...), custom_call_target="tpu_custom_call" | custom-call | tf_op jit(solution)/shard_map/first_layers/pallas_call | solution.py:384
  14.7 1.0 %third_layer.1 = bf16[16,8,8,64]{3,2,1,0:T(8,128)(2,1)} custom-call(bf16[2080,128]{1,0:T(8,128)(2,1)S(1)} %get-tuple-element.9.x3, bf16[128,1280]{1,0:T(8,128)(2,1)S(1)} %get-tuple-element.10.w3, f32[128,128]{1,0:T(8,128)S(1)} %get-tuple-element.11.bias3, bf16[16,4,8,64]{3,2,1,0:T(8,128)(2,1)S(1)} %get-tuple-element.12.upper), custom_call_target="tpu_custom_call" | custom-call | tf_op jit(solution)/shard_map/third_layer/pallas_call | solution.py:432

commit v11 on v3

--- a/solution.py
+++ b/solution.py
@@ -55,7 +55,7 @@
     return jnp.where(inside, 1.0, 0.0).astype(F32)
 
 
-def banded_weights(k1, k2, k3, stack1, base2, stack3, w1, w2, w3):
+def first_weights(k1, k2, stack1, base2, w1, w2):
     stack1[...] = jnp.zeros(stack1.shape, F32)
     for a in range(3):
         for b in range(3):
@@ -83,6 +83,8 @@
         both = [pltpu.roll(base, 8 * s, 1) if s else base for s in (y, min(y + 1, Y2 - 1))]
         w2[8 * y : 8 * y + 16, :] = jnp.concatenate(both, axis=0).astype(BF)
 
+
+def third_weights(k3, stack3, w3):
     stack3[...] = jnp.zeros(stack3.shape, F32)
     for n, (a, b, c) in enumerate(taps()):
         stack3[8 * n : 8 * n + 8, 0:16] = k3[a, b, c].astype(F32)
@@ -233,7 +235,7 @@
     def _(k):
         greet(g, lax.rem(t + k, strips))
 
-    pairs = [(sky.at[0], raw), (k1_in, k1), (k2_in, k2), (k3_in, k3), (b1_in, b1), (b2_in, b2), (b3_in, b3)]
+    pairs = [(k1_in, k1), (k2_in, k2), (sky.at[0], raw), (k3_in, k3), (b1_in, b1), (b2_in, b2), (b3_in, b3)]
     loads = [pltpu.make_async_copy(a, b, in_sem.at[n]) for n, (a, b) in enumerate(pairs)]
     for load in loads:
         load.start()
@@ -244,6 +246,9 @@
     moved[0:8, :] = jnp.zeros((8, 128), F32)
     moved[height : height + 16, :] = jnp.zeros((16, 128), F32)
     loads[0].wait()
+    loads[1].wait()
+    first_weights(k1, k2, stack1, base2, w1, w2)
+    loads[2].wait()
     values = jnp.dot(raw[...].astype(BF), order, preferred_element_type=F32)
     moved[4 : height + 4, :] = values
     slab[...] = moved[...].reshape(slab.shape).astype(BF)
@@ -275,7 +280,8 @@
         )
 
     def far(k):
-        strip = lax.rem(t + k, strips)
+        pair = k // 2
+        strip = lax.rem(pair, 2) * (strips // 2) + pair // 2 * 2 + lax.rem(k, 2)
         return pltpu.make_async_remote_copy(
             src_ref=slab.at[pl.ds(2 * strip, 3)],
             dst_ref=cube.at[far_plane],
@@ -297,9 +303,9 @@
 
     pltpu.make_async_copy(slab.at[pl.ds(2 * t, 3)], cube.at[plane], recv_sem.at[plane]).start()
 
-    for load in loads[1:]:
+    for load in loads[3:]:
         load.wait()
-    banded_weights(k1, k2, k3, stack1, base2, stack3, w1, w2, w3)
+    third_weights(k3, stack3, w3)
     for o in range(16):
         bias3[8 * o : 8 * o + 8, :] = jnp.full((8, 128), b3[o], F32)
 

time: 15.8 us -> 15.8 us (level)
  no operation moved by 1% of the time
where the time goes in v11:
time: 15.8 us; the launch traced here: 15.6 us
  Pallas kernels  15.6 us (99%)
    pallas_call x1, Pallas kernels, first_layers(): pl.pallas_call(spread_kernel, out_shape=[jax.ShapeDtypeStruct(X3_SHAPE, B...  14.6 us
    pallas_call x1, Pallas kernels, third_layer(): pl.pallas_call(third_kernel, out_shape=jax.ShapeDtypeStruct((16, half, ha...  1.03 us

profile of v11, /device:TPU:7, one launch (start us, length us, event | category | flops | bytes accessed | tf_op | source)
XLA Modules:
  0.0 15.6 jit_solution(10160030605884667642)
XLA Ops:
  0.0 14.6 %first_layers.1 = (bf16[2080,128]{1,0:T(8,128)(2,1)S(1)}, bf16[128,1280]{1,0:T(8,128)(2,1)S(1)}, f32[128,128]{1,0:T(8,128)S(1)}, bf16[16,4,8,64]{3,2,1,0:T(8,128)(2,1)S(1)}) custom-call(f32[1,256,128]{2,1,0:T(8,128)} %sky.1, bf16[1,3,3,3,8]{4,3,2,1,0:T(4,128)(2,1)} %bitcast.5, bf16[3,3,3,8,8]{4,3,2,1,0:T(8,128)(2,1)} %bitcast.3, ...), custom_call_target="tpu_custom_call" | custom-call | tf_op jit(solution)/shard_map/first_layers/pallas_call | solution.py:385
  14.6 1.0 %third_layer.1 = bf16[16,8,8,64]{3,2,1,0:T(8,128)(2,1)} custom-call(bf16[2080,128]{1,0:T(8,128)(2,1)S(1)} %get-tuple-element.9.x3, bf16[128,1280]{1,0:T(8,128)(2,1)S(1)} %get-tuple-element.10.w3, f32[128,128]{1,0:T(8,128)S(1)} %get-tuple-element.11.bias3, bf16[16,4,8,64]{3,2,1,0:T(8,128)(2,1)S(1)} %get-tuple-element.12.upper), custom_call_target="tpu_custom_call" | custom-call | tf_op jit(solution)/shard_map/third_layer/pallas_call | solution.py:433

commit v12 on v3

--- a/solution.py
+++ b/solution.py
@@ -255,14 +255,6 @@
     plane = 3 + t
     far_plane = jnp.where(low, SPAN + 3 + t, jnp.maximum(t - (strips - 3), 0))
 
-    @pl.when(beyond)
-    def _():
-        pl.semaphore_wait(barrier, 2 * strips - 1)
-
-    @pl.when(jnp.logical_not(beyond))
-    def _():
-        pl.semaphore_wait(barrier, strips - 1)
-
     def near(k):
         strip = lax.rem(t + k, strips)
         return pltpu.make_async_remote_copy(
@@ -275,7 +267,8 @@
         )
 
     def far(k):
-        strip = lax.rem(t + k, strips)
+        pair = k // 2
+        strip = lax.rem(pair, 2) * (strips // 2) + pair // 2 * 2 + lax.rem(k, 2)
         return pltpu.make_async_remote_copy(
             src_ref=slab.at[pl.ds(2 * strip, 3)],
             dst_ref=cube.at[far_plane],
@@ -285,23 +278,39 @@
             device_id_type=MESH,
         )
 
-    @pl.when(beyond)
-    def _():
-        @pl.loop(0, strips)
-        def _(k):
-            far(k).start()
-
-    @pl.loop(1, strips)
-    def _(k):
-        near(k).start()
-
-    pltpu.make_async_copy(slab.at[pl.ds(2 * t, 3)], cube.at[plane], recv_sem.at[plane]).start()
-
-    for load in loads[1:]:
-        load.wait()
-    banded_weights(k1, k2, k3, stack1, base2, stack3, w1, w2, w3)
-    for o in range(16):
-        bias3[8 * o : 8 * o + 8, :] = jnp.full((8, 128), b3[o], F32)
+    late = jnp.logical_and(jnp.logical_and(low, g > 0), lax.rem(g, 4) == 0)
+    expand_at = jnp.where(late, 0, 1)
+
+    @pl.loop(0, 2)
+    def _(turn):
+        @pl.when(turn == expand_at)
+        def _():
+            for load in loads[1:]:
+                load.wait()
+            banded_weights(k1, k2, k3, stack1, base2, stack3, w1, w2, w3)
+            for o in range(16):
+                bias3[8 * o : 8 * o + 8, :] = jnp.full((8, 128), b3[o], F32)
+
+        @pl.when(jnp.logical_and(turn == 0, beyond))
+        def _():
+            pl.semaphore_wait(barrier, 2 * strips - 1)
+
+            @pl.loop(0, strips)
+            def _(k):
+                far(k).start()
+
+        @pl.when(jnp.logical_and(turn == 0, jnp.logical_not(beyond)))
+        def _():
+            pl.semaphore_wait(barrier, strips - 1)
+
+        @pl.when(turn == 0)
+        def _():
+            @pl.loop(1, strips)
+            def _(k):
+                near(k).start()
+
+            own = slab.at[pl.ds(2 * t, 3)]
+            pltpu.make_async_copy(own, cube.at[plane], recv_sem.at[plane]).start()
 
     def arrived(p):
         pltpu.make_async_copy(cube.at[p], cube.at[p], recv_sem.at[p]).wait()

time: 15.8 us -> 15.2 us (0.962)
  Pallas kernels: 15.7 us -> 15.1 us
    pallas_call x1, Pallas kernels: 14.7 us -> 14 us  [first_layers(): pl.pallas_call(spread_kernel, out_shape=[jax.ShapeDtypeStruct(X3_SHAPE, B...]
where the time goes in v12:
time: 15.2 us; the launch traced here: 15.1 us
  Pallas kernels  15.1 us (99%)
    pallas_call x1, Pallas kernels, first_layers(): pl.pallas_call(spread_kernel, out_shape=[jax.ShapeDtypeStruct(X3_SHAPE, B...  14 us
    pallas_call x1, Pallas kernels, third_layer(): pl.pallas_call(third_kernel, out_shape=jax.ShapeDtypeStruct((16, half, ha...  1.02 us

profile of v12, /device:TPU:7, one launch (start us, length us, event | category | flops | bytes accessed | tf_op | source)
XLA Modules:
  0.0 15.1 jit_solution(3661157709923584833)
XLA Ops:
  0.0 14.0 %first_layers.1 = (bf16[2080,128]{1,0:T(8,128)(2,1)S(1)}, bf16[128,1280]{1,0:T(8,128)(2,1)S(1)}, f32[128,128]{1,0:T(8,128)S(1)}, bf16[16,4,8,64]{3,2,1,0:T(8,128)(2,1)S(1)}) custom-call(f32[1,256,128]{2,1,0:T(8,128)} %sky.1, bf16[1,3,3,3,8]{4,3,2,1,0:T(4,128)(2,1)} %bitcast.5, bf16[3,3,3,8,8]{4,3,2,1,0:T(8,128)(2,1)} %bitcast.3, ...), custom_call_target="tpu_custom_call" | custom-call | tf_op jit(solution)/shard_map/first_layers/pallas_call | solution.py:388
  14.0 1.0 %third_layer.1 = bf16[16,8,8,64]{3,2,1,0:T(8,128)(2,1)} custom-call(bf16[2080,128]{1,0:T(8,128)(2,1)S(1)} %get-tuple-element.9.x3, bf16[128,1280]{1,0:T(8,128)(2,1)S(1)} %get-tuple-element.10.w3, f32[128,128]{1,0:T(8,128)S(1)} %get-tuple-element.11.bias3, bf16[16,4,8,64]{3,2,1,0:T(8,128)(2,1)S(1)} %get-tuple-element.12.upper), custom_call_target="tpu_custom_call" | custom-call | tf_op jit(solution)/shard_map/third_layer/pallas_call | solution.py:436

commit v13 on v12

--- a/solution.py
+++ b/solution.py
@@ -268,7 +268,9 @@
 
     def far(k):
         pair = k // 2
-        strip = lax.rem(pair, 2) * (strips // 2) + pair // 2 * 2 + lax.rem(k, 2)
+        far_z = jnp.logical_or(pair == 1, pair >= 5)
+        y = pair - jnp.where(pair >= 5, 4, jnp.where(pair >= 1, 1, 0))
+        strip = jnp.where(far_z, strips // 2, 0) + 2 * y + lax.rem(k, 2)
         return pltpu.make_async_remote_copy(
             src_ref=slab.at[pl.ds(2 * strip, 3)],
             dst_ref=cube.at[far_plane],

time: 15.2 us -> 15.2 us (level)
  no operation moved by 1% of the time
where the time goes in v13:
time: 15.2 us; the launch traced here: 15.1 us
  Pallas kernels  15.1 us (99%)
    pallas_call x1, Pallas kernels, first_layers(): pl.pallas_call(spread_kernel, out_shape=[jax.ShapeDtypeStruct(X3_SHAPE, B...  14 us
    pallas_call x1, Pallas kernels, third_layer(): pl.pallas_call(third_kernel, out_shape=jax.ShapeDtypeStruct((16, half, ha...  1.02 us

profile of v13, /device:TPU:7, one launch (start us, length us, event | category | flops | bytes accessed | tf_op | source)
XLA Modules:
  0.0 15.1 jit_solution(14216698931403239399)
XLA Ops:
  0.0 14.0 %first_layers.1 = (bf16[2080,128]{1,0:T(8,128)(2,1)S(1)}, bf16[128,1280]{1,0:T(8,128)(2,1)S(1)}, f32[128,128]{1,0:T(8,128)S(1)}, bf16[16,4,8,64]{3,2,1,0:T(8,128)(2,1)S(1)}) custom-call(f32[1,256,128]{2,1,0:T(8,128)} %sky.1, bf16[1,3,3,3,8]{4,3,2,1,0:T(4,128)(2,1)} %bitcast.5, bf16[3,3,3,8,8]{4,3,2,1,0:T(8,128)(2,1)} %bitcast.3, ...), custom_call_target="tpu_custom_call" | custom-call | tf_op jit(solution)/shard_map/first_layers/pallas_call | solution.py:390
  14.0 1.0 %third_layer.1 = bf16[16,8,8,64]{3,2,1,0:T(8,128)(2,1)} custom-call(bf16[2080,128]{1,0:T(8,128)(2,1)S(1)} %get-tuple-element.9.x3, bf16[128,1280]{1,0:T(8,128)(2,1)S(1)} %get-tuple-element.10.w3, f32[128,128]{1,0:T(8,128)S(1)} %get-tuple-element.11.bias3, bf16[16,4,8,64]{3,2,1,0:T(8,128)(2,1)S(1)} %get-tuple-element.12.upper), custom_call_target="tpu_custom_call" | custom-call | tf_op jit(solution)/shard_map/third_layer/pallas_call | solution.py:438

commit v14 on v13

--- a/solution.py
+++ b/solution.py
@@ -297,9 +297,11 @@
         def _():
             pl.semaphore_wait(barrier, 2 * strips - 1)
 
-            @pl.loop(0, strips)
-            def _(k):
-                far(k).start()
+            @pl.when(jnp.logical_not(late))
+            def _():
+                @pl.loop(0, strips)
+                def _(k):
+                    far(k).start()
 
         @pl.when(jnp.logical_and(turn == 0, jnp.logical_not(beyond)))
         def _():
@@ -313,6 +315,12 @@
 
             own = slab.at[pl.ds(2 * t, 3)]
             pltpu.make_async_copy(own, cube.at[plane], recv_sem.at[plane]).start()
+
+            @pl.when(late)
+            def _():
+                @pl.loop(0, strips)
+                def _(k):
+                    far(k).start()
 
     def arrived(p):
         pltpu.make_async_copy(cube.at[p], cube.at[p], recv_sem.at[p]).wait()

time: 15.2 us -> 15.2 us (level)
  no operation moved by 1% of the time
where the time goes in v14:
time: 15.2 us; the launch traced here: 15.1 us
  Pallas kernels  15.1 us (99%)
    pallas_call x1, Pallas kernels, first_layers(): pl.pallas_call(spread_kernel, out_shape=[jax.ShapeDtypeStruct(X3_SHAPE, B...  14.1 us
    pallas_call x1, Pallas kernels, third_layer(): pl.pallas_call(third_kernel, out_shape=jax.ShapeDtypeStruct((16, half, ha...  1.02 us

profile of v14, /device:TPU:7, one launch (start us, length us, event | category | flops | bytes accessed | tf_op | source)
XLA Modules:
  0.0 15.1 jit_solution(8065662916979801655)
XLA Ops:
  0.0 14.1 %first_layers.1 = (bf16[2080,128]{1,0:T(8,128)(2,1)S(1)}, bf16[128,1280]{1,0:T(8,128)(2,1)S(1)}, f32[128,128]{1,0:T(8,128)S(1)}, bf16[16,4,8,64]{3,2,1,0:T(8,128)(2,1)S(1)}) custom-call(f32[1,256,128]{2,1,0:T(8,128)} %sky.1, bf16[1,3,3,3,8]{4,3,2,1,0:T(4,128)(2,1)} %bitcast.5, bf16[3,3,3,8,8]{4,3,2,1,0:T(8,128)(2,1)} %bitcast.3, ...), custom_call_target="tpu_custom_call" | custom-call | tf_op jit(solution)/shard_map/first_layers/pallas_call | solution.py:398
  14.1 1.0 %third_layer.1 = bf16[16,8,8,64]{3,2,1,0:T(8,128)(2,1)} custom-call(bf16[2080,128]{1,0:T(8,128)(2,1)S(1)} %get-tuple-element.9.x3, bf16[128,1280]{1,0:T(8,128)(2,1)S(1)} %get-tuple-element.10.w3, f32[128,128]{1,0:T(8,128)S(1)} %get-tuple-element.11.bias3, bf16[16,4,8,64]{3,2,1,0:T(8,128)(2,1)S(1)} %get-tuple-element.12.upper), custom_call_target="tpu_custom_call" | custom-call | tf_op jit(solution)/shard_map/third_layer/pallas_call | solution.py:446
